TPU v7x, 32 devices: a whole 2x2x4 slice. The times are simulated.
32 devices in a mesh: gx: 4 (over y, x), gy: 8 (over z, core).
Axes of the slice: x: 2, y: 2, z: 4, core: 2. Of those that a mesh axis runs over, the one named last changes fastest.
Arguments:
- features: bfloat16 [4, 8, 512, 128], P('gx', 'gy'), may hold values from -6 to 6
- coords: float32 [4, 8, 3, 512], P('gx', 'gy'), may hold values from 0 to 1
- migrate_x_slots: int32 [4, 8, 2, 32], P('gx', 'gy'), may hold values from 0 to 511, as said below
- migrate_y_slots: int32 [4, 8, 2, 32], P('gx', 'gy'), may hold values from 0 to 511, as said below
- ghost_slots: int32 [4, 8, 256], P('gx', 'gy'), may hold values from 0 to 511, as said below
- neighbours: int32 [4, 8, 512, 16], P('gx', 'gy'), may hold values from 0 to 2815, as said below
- source_weight: bfloat16 [128, 128], replicated, may hold values from -0.5 to 0.5
- target_weight: bfloat16 [128, 128], replicated, may hold values from -0.5 to 0.5
- radial_weight: float32 [8, 128], replicated, may hold values from -2 to 2
- environ_first: bfloat16 [128, 128], replicated, may hold values from -0.5 to 0.5
- mixing_first: bfloat16 [128, 128], replicated, may hold values from -0.5 to 0.5
- coupler_first: bfloat16 [128, 128], replicated, may hold values from -0.5 to 0.5
- environ_second: bfloat16 [128, 128], replicated, may hold values from -0.5 to 0.5
- mixing_second: bfloat16 [128, 128], replicated, may hold values from -0.5 to 0.5
- coupler_second: bfloat16 [128, 128], replicated, may hold values from -0.5 to 0.5
- readout: bfloat16 [128], replicated, may hold values from -0.5 to 0.5
Outputs:
- forces: float32 [4, 8, 3, 512], P('gx', 'gy')
- energies: float32 [4, 8, 512], P('gx', 'gy')
Inputs may be any that keep to these rules, and one draw needn't show every extreme that they name: `migrate_x_slots`: in each device's two rows the 64 slots are distinct. `migrate_y_slots`: in each device's two rows the 64 slots are distinct. `ghost_slots`: each device's 256 slots are distinct. `neighbours`: an entry of atom i is either a slot of the same device other than i, or 512 + s * 256 + g with s in 0..8 but never 4 and g below 256, naming ghost g of the device at grid offset (s // 3 - 1, s % 3 - 1), periodic.
All inputs are finite; a program needn't handle non-finite values.
Results may differ from a plain program's by a relative error of at most 0.005.
Values may be sent and summed in bfloat16 or wider, within the bound.
A program may use at most 64 MiB of HBM per device.

v0:
```python
import math

import jax
import jax.numpy as jnp
from jax import lax
from jax.sharding import PartitionSpec as P

soften = 0.25
cutoff = 2.0


def from_behind(value, axis, steps):
    count = lax.axis_size(axis)
    pairs = [(source, (source + steps) % count) for source in range(count)]
    return lax.ppermute(value, axis, pairs)


def extended(shard, sides, width):
    for axis, dim in sides:
        count, length = (lax.axis_size(axis), shard.shape[dim])
        up = [(i, (i + 1) % count) for i in range(count)]
        down = [(j, i) for i, j in up]
        last = lax.slice_in_dim(shard, length - width, length, axis=dim)
        first = lax.slice_in_dim(shard, 0, width, axis=dim)
        before = lax.ppermute(last, axis, up)
        after = lax.ppermute(first, axis, down)
        shard = jnp.concatenate([before, shard, after], axis=dim)
    return shard


def block_energy(
    positions,
    first_row,
    neighbour_block,
    source_block,
    target_table,
    radial_weight,
    layers,
    readout,
):
    block_rows, slots_per = neighbour_block.shape
    breadth = target_table.shape[1]
    flat_index = neighbour_block.reshape(block_rows * slots_per)
    pos_own = lax.dynamic_slice_in_dim(positions, first_row, block_rows, 1)
    pos_far = jnp.take(positions, flat_index, axis=1).reshape(3, block_rows, slots_per)
    offset = pos_far - pos_own[:, :, None]
    length = jnp.sqrt(jnp.sum(offset * offset, axis=0) + soften)
    direction = offset / length[None]
    scaled = length / cutoff
    smooth = (1.0 - scaled * scaled) ** 2
    frequency = (jnp.arange(radial_weight.shape[0]) + 1).astype(jnp.float32) * math.pi
    bessel = jnp.sin(scaled[:, :, None] * frequency) / length[:, :, None] * smooth[:, :, None]
    radial = jnp.einsum("rnb,bc->rnc", bessel, radial_weight, precision=lax.Precision.HIGHEST)
    gathered = jnp.take(target_table, flat_index, axis=0).reshape(block_rows, slots_per, breadth)
    paired = source_block.astype(jnp.float32)[:, None, :] + gathered.astype(jnp.float32) + radial
    hidden = jax.nn.silu(paired).reshape(block_rows * slots_per, breadth).astype(jnp.bfloat16)
    weighted = direction * smooth[None]
    norm_scale = 1.0 / math.sqrt(slots_per)
    latent = None
    for environ, mixing, coupler in layers:
        carried = jnp.dot(hidden, environ, preferred_element_type=jnp.float32).reshape(
            block_rows, slots_per, breadth
        )
        environment = [jnp.sum(weighted[k][:, :, None] * carried, axis=1) for k in range(3)]
        coupled = direction[0][:, :, None] * environment[0][:, None, :]
        coupled = coupled + direction[1][:, :, None] * environment[1][:, None, :]
        coupled = coupled + direction[2][:, :, None] * environment[2][:, None, :]
        coupled = (
            (coupled * norm_scale).reshape(block_rows * slots_per, breadth).astype(jnp.bfloat16)
        )
        mixed = jnp.dot(hidden, mixing, preferred_element_type=jnp.float32) + jnp.dot(
            coupled, coupler, preferred_element_type=jnp.float32
        )
        latent = jax.nn.silu(mixed)
        hidden = latent.astype(jnp.bfloat16)
    edge_energy = (
        jnp.sum(latent * readout.astype(jnp.float32)[None, :], axis=1).reshape(
            block_rows, slots_per
        )
        * smooth
    )
    atom_energy = jnp.sum(edge_energy, axis=1)
    return (jnp.sum(atom_energy), atom_energy)


def device_forces(positions, neighbours, source_rows, target_table, radial_weight, layers, readout):
    atom_count = neighbours.shape[0]
    block_atoms = math.gcd(atom_count, 256)
    block_count = atom_count // block_atoms

    def advance(total, block_number):
        first_row = block_number * block_atoms
        neighbour_block = lax.dynamic_slice_in_dim(neighbours, first_row, block_atoms, 0)
        source_block = lax.dynamic_slice_in_dim(source_rows, first_row, block_atoms, 0)

        def energy_of(table_pos):
            return block_energy(
                table_pos,
                first_row,
                neighbour_block,
                source_block,
                target_table,
                radial_weight,
                layers,
                readout,
            )

        gradient, atom_energy = jax.grad(energy_of, has_aux=True)(positions)
        return (total + gradient, atom_energy)

    total, energies = lax.scan(
        advance, jnp.zeros(positions.shape, jnp.float32), jnp.arange(block_count, dtype=jnp.int32)
    )
    return (total, energies.reshape(atom_count))


def move_along_x(own_rows, own_coords, slots):
    for column, stride in ((0, 1), (1, -1)):
        picked = slots[column]
        arrived_rows = from_behind(own_rows[picked], "gx", stride)
        arrived_coords = from_behind(own_coords[:, picked], "gx", stride)
        own_rows = own_rows.at[picked].set(arrived_rows)
        own_coords = own_coords.at[:, picked].set(arrived_coords)
    return (own_rows, own_coords)


def move_along_y(own_rows, own_coords, slots):
    for column, stride in ((0, 1), (1, -1)):
        picked = slots[column]
        arrived_rows = from_behind(own_rows[picked], "gy", stride)
        arrived_coords = from_behind(own_coords[:, picked], "gy", stride)
        own_rows = own_rows.at[picked].set(arrived_rows)
        own_coords = own_coords.at[:, picked].set(arrived_coords)
    return (own_rows, own_coords)


def fold_back(ghost_grad):
    partial_sum = ghost_grad[:, :, 1]
    for column, stride in ((0, -1), (2, 1)):
        partial_sum = partial_sum + from_behind(ghost_grad[:, :, column], "gy", stride)
    whole = partial_sum[:, 1]
    for column, stride in ((0, -1), (2, 1)):
        whole = whole + from_behind(partial_sum[:, column], "gx", stride)
    return whole


def per_device(
    features,
    coords,
    migrate_x_slots,
    migrate_y_slots,
    ghost_slots,
    neighbours,
    source_weight,
    target_weight,
    radial_weight,
    environ_first,
    mixing_first,
    coupler_first,
    environ_second,
    mixing_second,
    coupler_second,
    readout,
):
    own_rows = features[0, 0]
    own_coords = coords[0, 0]
    own_rows, own_coords = move_along_x(own_rows, own_coords, migrate_x_slots[0, 0])
    own_rows, own_coords = move_along_y(own_rows, own_coords, migrate_y_slots[0, 0])
    atom_count = own_rows.shape[0]
    ghosts = ghost_slots[0, 0]
    ghost_count = ghosts.shape[0]
    ghost_coords = own_coords[:, ghosts]
    source_rows = jnp.dot(own_rows, source_weight, preferred_element_type=jnp.float32).astype(
        jnp.bfloat16
    )
    payload = own_rows[ghosts]
    breadth = payload.shape[1]
    halo_rows = extended(payload[None, None], (("gx", 0), ("gy", 1)), 1)
    halo_coords = extended(ghost_coords[None, None], (("gx", 0), ("gy", 1)), 1)
    stacked = jnp.concatenate([own_rows, halo_rows.reshape(9 * ghost_count, breadth)], axis=0)
    target_table = jnp.dot(stacked, target_weight, preferred_element_type=jnp.float32).astype(
        jnp.bfloat16
    )
    positions = jnp.concatenate(
        [own_coords, jnp.moveaxis(halo_coords, 2, 0).reshape(3, 9 * ghost_count)], axis=1
    )
    layers = (
        (environ_first, mixing_first, coupler_first),
        (environ_second, mixing_second, coupler_second),
    )
    gradient, energies = device_forces(
        positions, neighbours[0, 0], source_rows, target_table, radial_weight, layers, readout
    )
    returned = fold_back(gradient[:, atom_count:].reshape(3, 3, 3, ghost_count))
    total = gradient[:, :atom_count].at[:, ghosts].add(returned)
    return ((-total)[None, None], energies[None, None])


def solution(mesh):
    in_specs = (
        P("gx", "gy", None, None),
        P("gx", "gy", None, None),
        P("gx", "gy", None, None),
        P("gx", "gy", None, None),
        P("gx", "gy", None),
        P("gx", "gy", None, None),
        P(),
        P(),
        P(),
        P(),
        P(),
        P(),
        P(),
        P(),
        P(),
        P(),
    )
    out_specs = (P("gx", "gy", None, None), P("gx", "gy", None))
    return jax.shard_map(
        per_device, mesh=mesh, in_specs=in_specs, out_specs=out_specs, check_vma=False
    )
```

profile of v0, /device:TPU:0, one launch (start us, length us, event | category | flops | bytes accessed | tf_op | source)
XLA Modules:
  0.0 487.7 jit_solution(5684829582457187973)
XLA Ops:
  13.6 3.7 collective-permute-done.1
  18.7 4.9 %collective-permute-done.2 = f32[3,32]{0,1:T(8,128)S(1)} collective-permute-done((f32[3,32]{0,1:T(8,128)S(1)}, f32[3,32]{0,1:T(8,128)S(1)}, u32[]{:S(2)}, u32[]{:S(2)}) %collective-permute-start.2) | collective-permute-done | bytes 416 | tf_op jit(solution)/shard_map/ppermute | solution.py:15
  34.1 3.2 collective-permute-done.4
  42.2 4.8 collective-permute-done.7
  67.5 3.7 collective-permute-done.14
  71.6 393.7 %while.13 = (s32[]{:T(128)}, f32[3,2816]{0,1:T(8,128)}, f32[2,256]{1,0:T(2,128)}, s32[2]{0:T(128)S(1)}, s32[512,16]{1,0:T(8,128)S(1)}, /*index=5*/f32[3,2816]{0,...) while((s32[]{:T(128)}, f32[3,2816]{0,1:T(8,128)}, ...), condition=%wide.region_43.44_spmd.clone, body=%wide.region_8.43_spmd.clone.sunk | while | flops 1787323520 | bytes 173143504 | solution.py:111
  76.3 14.9 %gather_fusion.1 = bf16[4096,128]{1,0:T(8,128)(2,1)} fusion(bf16[2816,128]{1,0:T(8,128)(2,1)S(1)} %get-tuple-element.624, s32[4096]{0:T(1024)S(1)} %broadcast_clamp_fusion.2), kind=kCustom, calls=%fused_computation.1.clone.clone.1 | custom fusion | bytes 2113536 | tf_op jit(solution)/shard_map/while/body/eval_jaxpr/jvp(jit(_take))/gather | solution.py:54
  91.2 12.1 %gather_fusion = f32[4096,3]{1,0:T(8,128)S(1)} fusion(f32[3,2816]{0,1:T(8,128)} %get-tuple-element.621, s32[4096]{0:T(1024)S(1)} %broadcast_clamp_fusion.2), kind=kCustom, calls=%fused_computation.clone.clone.1 | custom fusion | bytes 114688 | tf_op jit(solution)/shard_map/while/body/eval_jaxpr/jvp(jit(_take))/gather | solution.py:45
  113.0 6.0 %multiply_convert_fusion.4 = (bf16[256,16,128]{2,0,1:T(8,128)(2,1)S(1)}, f32[256,16,128]{2,0,1:T(8,128)}) fusion(f32[8,128]{1,0:T(8,128)S(1)} %copy-done.65, f32[256,16]{0,1:T(8,128)S(1)} %get-tuple-element.514, f32[256,16]{0,1:T(8,128)S(1)} %copy.387, f32[8]{0:T(128)S(1)} %copy-done.71, f32[256,16]{0,1:T(8,128)S(1)} %get-tuple-element.515, ...), kind=kOutput, calls=%fused_computation.119.clone.1 | convolution fusion | flops 55148544 | bytes 4382752 | tf_op jit(solution)/shard_map/while/body/eval_jaxpr/jvp(rnb,bc->rnc)/dot_general | solution.py:53
  157.6 3.1 fusion.205
  164.4 3.5 multiply_reduce_fusion.32
  174.7 20.3 %fusion.207 = f32[256,16,128]{2,1,0:T(8,128)S(1)} fusion(f32[256,16,128]{2,1,0:T(8,128)S(1)} %bitcast.387, f32[256,16]{1,0:T(8,128)S(1)} %copy.404), kind=kOutput, calls=%fused_computation.22.clone.1 | output fusion | flops 557071 | bytes 4210688 | tf_op jit(solution)/shard_map/while/body/eval_jaxpr/transpose(jvp())/broadcast_in_dim | solution.py:64
  195.1 20.4 %fusion.206 = f32[256,16,128]{2,1,0:T(8,128)S(1)} fusion(f32[256,16,128]{2,1,0:T(8,128)S(1)} %bitcast.388, f32[256,16]{1,0:T(8,128)S(1)} %copy.403), kind=kOutput, calls=%fused_computation.23.clone.1 | output fusion | flops 557071 | bytes 4210688 | tf_op jit(solution)/shard_map/while/body/eval_jaxpr/transpose(jvp())/broadcast_in_dim | solution.py:64
  237.3 3.4 fusion.216
  243.2 23.0 %scatter_custom_fusion.20 = f32[3,2816]{0,1:T(8,128)S(1)} fusion(s32[4096]{0:T(1024)} %bitcast.407, f32[4096,3]{1,0:T(8,128)} %copy.428, f32[]{:T(128)} %constant.21.clone.45..sunk), kind=kCustom, calls=%fused_computation.127.clone.1 | custom fusion | flops 12288 | bytes 34304 | tf_op jit(solution)/shard_map/while/body/eval_jaxpr/transpose(jvp(jit(_take)))/scatter-add | solution.py:45
  272.4 14.9 %gather_fusion.1 = bf16[4096,128]{1,0:T(8,128)(2,1)} fusion(bf16[2816,128]{1,0:T(8,128)(2,1)S(1)} %get-tuple-element.624, s32[4096]{0:T(1024)S(1)} %broadcast_clamp_fusion.2), kind=kCustom, calls=%fused_computation.1.clone.clone.1 | custom fusion | bytes 2113536 | tf_op jit(solution)/shard_map/while/body/eval_jaxpr/jvp(jit(_take))/gather | solution.py:54
  287.3 12.1 %gather_fusion = f32[4096,3]{1,0:T(8,128)S(1)} fusion(f32[3,2816]{0,1:T(8,128)} %get-tuple-element.621, s32[4096]{0:T(1024)S(1)} %broadcast_clamp_fusion.2), kind=kCustom, calls=%fused_computation.clone.clone.1 | custom fusion | bytes 114688 | tf_op jit(solution)/shard_map/while/body/eval_jaxpr/jvp(jit(_take))/gather | solution.py:45
  309.1 6.0 %multiply_convert_fusion.4 = (bf16[256,16,128]{2,0,1:T(8,128)(2,1)S(1)}, f32[256,16,128]{2,0,1:T(8,128)}) fusion(f32[8,128]{1,0:T(8,128)S(1)} %copy-done.65, f32[256,16]{0,1:T(8,128)S(1)} %get-tuple-element.514, f32[256,16]{0,1:T(8,128)S(1)} %copy.387, f32[8]{0:T(128)S(1)} %copy-done.71, f32[256,16]{0,1:T(8,128)S(1)} %get-tuple-element.515, ...), kind=kOutput, calls=%fused_computation.119.clone.1 | convolution fusion | flops 55148544 | bytes 4382752 | tf_op jit(solution)/shard_map/while/body/eval_jaxpr/jvp(rnb,bc->rnc)/dot_general | solution.py:53
  360.5 3.5 multiply_reduce_fusion.32
  370.8 20.3 %fusion.207 = f32[256,16,128]{2,1,0:T(8,128)S(1)} fusion(f32[256,16,128]{2,1,0:T(8,128)S(1)} %bitcast.387, f32[256,16]{1,0:T(8,128)S(1)} %copy.404), kind=kOutput, calls=%fused_computation.22.clone.1 | output fusion | flops 557071 | bytes 4210688 | tf_op jit(solution)/shard_map/while/body/eval_jaxpr/transpose(jvp())/broadcast_in_dim | solution.py:64
  391.1 20.4 %fusion.206 = f32[256,16,128]{2,1,0:T(8,128)S(1)} fusion(f32[256,16,128]{2,1,0:T(8,128)S(1)} %bitcast.388, f32[256,16]{1,0:T(8,128)S(1)} %copy.403), kind=kOutput, calls=%fused_computation.23.clone.1 | output fusion | flops 557071 | bytes 4210688 | tf_op jit(solution)/shard_map/while/body/eval_jaxpr/transpose(jvp())/broadcast_in_dim | solution.py:64
  433.4 3.4 fusion.216
  439.3 23.0 %scatter_custom_fusion.20 = f32[3,2816]{0,1:T(8,128)S(1)} fusion(s32[4096]{0:T(1024)} %bitcast.407, f32[4096,3]{1,0:T(8,128)} %copy.428, f32[]{:T(128)} %constant.21.clone.45..sunk), kind=kCustom, calls=%fused_computation.127.clone.1 | custom fusion | flops 12288 | bytes 34304 | tf_op jit(solution)/shard_map/while/body/eval_jaxpr/transpose(jvp(jit(_take)))/scatter-add | solution.py:45
  467.3 8.8 %collective-permute-done.16 = f32[3,3,256]{0,2,1:T(8,128)S(1)} collective-permute-done((f32[3,3,256]{0,2,1:T(8,128)S(1)}, f32[3,3,256]{0,2,1:T(8,128)S(1)}, u32[]{:S(2)}, u32[]{:S(2)}) %collective-permute-start.16) | collective-permute-done | bytes 9248 | tf_op jit(solution)/shard_map/ppermute | solution.py:15
  (595 shorter events, 243.6 us)
Async XLA Ops:
  0.6 70.6 %copy-start = (bf16[128,128]{1,0:T(8,128)(2,1)S(1)}, bf16[128,128]{1,0:T(8,128)(2,1)}, u32[]{:S(2)}) copy-start(bf16[128,128]{1,0:T(8,128)(2,1)} %param.25) | copy-start | bytes 98308
  0.6 41.1 %copy-start.57 = (s32[1,1,512,16]{2,3,1,0:T(8,128)S(1)}, s32[1,1,512,16]{2,3,1,0:T(8,128)}, u32[]{:S(2)}) copy-start(s32[1,1,512,16]{2,3,1,0:T(8,128)} %param.23) | copy-start | bytes 98308
  0.7 40.4 %copy-start.59 = (bf16[128,128]{1,0:T(8,128)(2,1)S(1)}, bf16[128,128]{1,0:T(8,128)(2,1)}, u32[]{:S(2)}) copy-start(bf16[128,128]{1,0:T(8,128)(2,1)} %param.27) | copy-start | bytes 98308
  3.0 27.1 %collective-permute-start.8 = (bf16[32,128]{1,0:T(8,128)(2,1)S(1)}, bf16[32,128]{1,0:T(8,128)(2,1)S(1)}, u32[]{:S(2)}, u32[]{:S(2)}) collective-permute-start(bf16[32,128]{1,0:T(8,128)(2,1)S(1)} %gather_fusion.7), channel_id=1, source_target_pairs={{0,8},{8,16},{16,24},{24,0},{1,9},{9,17},{17,25},{25,1},{2,10},{10... | collective-permute-start | bytes 24584 | tf_op jit(solution)/shard_map/ppermute | solution.py:15
  7.4 4.7 collective-permute-start
  13.4 3.8 collective-permute-start.1
  18.6 5.0 %collective-permute-start.2 = (f32[3,32]{0,1:T(8,128)S(1)}, f32[3,32]{0,1:T(8,128)S(1)}, u32[]{:S(2)}, u32[]{:S(2)}) collective-permute-start(f32[3,32]{0,1:T(8,128)S(1)} %bitcast.422), channel_id=1, source_target_pairs={{0,1},{1,2},{2,3},{3,4},{4,5},{5,6},{6,7},{7,0},{8,9},{9,10},{10,1... | collective-permute-start | bytes 1160 | tf_op jit(solution)/shard_map/ppermute | solution.py:15
  25.0 1.5 collective-permute-start.3
  28.0 6.0 %collective-permute-start.5 = (f32[1,1,3,256]{2,3,1,0:T(8,128)S(1)}, f32[1,1,3,256]{2,3,1,0:T(8,128)S(1)}, u32[]{:S(2)}, u32[]{:S(2)}) collective-permute-start(f32[1,1,3,256]{2,3,1,0:T(8,128)S(1)} %bitcast.415), channel_id=1, source_target_pairs={{8,0},{16,8},{24,16},{0,24},{9,1},{17,9},{25,17},{1,25},{10,2},{18... | collective-permute-start | bytes 9224 | tf_op jit(solution)/shard_map/ppermute | solution.py:26
  29.0 8.2 %collective-permute-start.4 = (f32[1,1,3,256]{2,3,1,0:T(8,128)S(1)}, f32[1,1,3,256]{2,3,1,0:T(8,128)S(1)}, u32[]{:S(2)}, u32[]{:S(2)}) collective-permute-start(f32[1,1,3,256]{2,3,1,0:T(8,128)S(1)} %bitcast.416), channel_id=1, source_target_pairs={{0,8},{8,16},{16,24},{24,0},{1,9},{9,17},{17,25},{25,1},{2,10},{10... | collective-permute-start | bytes 9224 | tf_op jit(solution)/shard_map/ppermute | solution.py:25
  31.5 8.1 %collective-permute-start.9 = (bf16[32,128]{1,0:T(8,128)(2,1)S(1)}, bf16[32,128]{1,0:T(8,128)(2,1)S(1)}, u32[]{:S(2)}, u32[]{:S(2)}) collective-permute-start(bf16[32,128]{1,0:T(8,128)(2,1)S(1)} %gather_fusion.8), channel_id=1, source_target_pairs={{0,24},{8,0},{16,8},{24,16},{1,25},{9,1},{17,9},{25,17},{2,26},{10... | collective-permute-start | bytes 24584 | tf_op jit(solution)/shard_map/ppermute | solution.py:15
  37.2 9.7 %collective-permute-start.7 = (f32[3,1,3,256]{2,3,1,0:T(8,128)S(1)}, f32[3,1,3,256]{2,3,1,0:T(8,128)S(1)}, u32[]{:S(2)}, u32[]{:S(2)}) collective-permute-start(f32[3,1,3,256]{2,3,1,0:T(8,128)S(1)} %pad_maximum_fusion.1), channel_id=1, source_target_pairs={{1,0},{2,1},{3,2},{4,3},{5,4},{6,5},{7,6},{0,7},{9,8},{10,9},{11,1... | collective-permute-start | bytes 27656 | tf_op jit(solution)/shard_map/ppermute | solution.py:26
  39.6 10.4 %collective-permute-start.6 = (f32[3,1,3,256]{2,3,1,0:T(8,128)S(1)}, f32[3,1,3,256]{2,3,1,0:T(8,128)S(1)}, u32[]{:S(2)}, u32[]{:S(2)}) collective-permute-start(f32[3,1,3,256]{2,3,1,0:T(8,128)S(1)} %pad_maximum_fusion.1), channel_id=1, source_target_pairs={{0,1},{1,2},{2,3},{3,4},{4,5},{5,6},{6,7},{7,0},{8,9},{9,10},{10,1... | collective-permute-start | bytes 27656 | tf_op jit(solution)/shard_map/ppermute | solution.py:25
  41.0 9.2 %collective-permute-start.10 = (bf16[32,128]{1,0:T(8,128)(2,1)S(1)}, bf16[32,128]{1,0:T(8,128)(2,1)S(1)}, u32[]{:S(2)}, u32[]{:S(2)}) collective-permute-start(bf16[32,128]{1,0:T(8,128)(2,1)S(1)} %gather_fusion.9), channel_id=1, source_target_pairs={{0,1},{1,2},{2,3},{3,4},{4,5},{5,6},{6,7},{7,0},{8,9},{9,10},{10,1... | collective-permute-start | bytes 24584 | tf_op jit(solution)/shard_map/ppermute | solution.py:15
  51.6 2.3 collective-permute-start.11
  55.5 4.5 collective-permute-start.13
  56.9 5.2 %collective-permute-start.12 = (bf16[1,1,256,128]{3,2,1,0:T(8,128)(2,1)S(1)}, bf16[1,1,256,128]{3,2,1,0:T(8,128)(2,1)S(1)}, u32[]{:S(2)}, u32[]{:S(2)}) collective-permute-start(bf16[1,1,256,128]{3,2,1,0:T(8,128)(2,1)S(1)} %bitcast.411), channel_id=1, source_target_pairs={{0,8},{8,16},{16,24},{24,0},{1,9},{9,17},{17,25},{25,1},{2,10},{10... | collective-permute-start | bytes 196616 | tf_op jit(solution)/shard_map/ppermute | solution.py:25
  62.1 5.3 %collective-permute-start.15 = (bf16[3,1,256,128]{3,2,1,0:T(8,128)(2,1)S(1)}, bf16[3,1,256,128]{3,2,1,0:T(8,128)(2,1)S(1)}, u32[]{:S(2)}, u32[]{:S(2)}) collective-permute-start(bf16[3,1,256,128]{3,2,1,0:T(8,128)(2,1)S(1)} %pad_maximum_fusion.2), channel_id=1, source_target_pairs={{1,0},{2,1},{3,2},{4,3},{5,4},{6,5},{7,6},{0,7},{9,8},{10,9},{11,1... | collective-permute-start | bytes 589832 | tf_op jit(solution)/shard_map/ppermute | solution.py:26
  64.3 6.9 %collective-permute-start.14 = (bf16[3,1,256,128]{3,2,1,0:T(8,128)(2,1)S(1)}, bf16[3,1,256,128]{3,2,1,0:T(8,128)(2,1)S(1)}, u32[]{:S(2)}, u32[]{:S(2)}) collective-permute-start(bf16[3,1,256,128]{3,2,1,0:T(8,128)(2,1)S(1)} %pad_maximum_fusion.2), channel_id=1, source_target_pairs={{0,1},{1,2},{2,3},{3,4},{4,5},{5,6},{6,7},{7,0},{8,9},{9,10},{10,1... | collective-permute-start | bytes 589832 | tf_op jit(solution)/shard_map/ppermute | solution.py:25
  75.2 31.9 %copy-start.38 = (f32[3,256]{1,0:T(4,128)}, f32[3,256]{1,0:T(4,128)S(1)}, u32[]{:S(2)}) copy-start(f32[3,256]{1,0:T(4,128)S(1)} %copy.390) | copy-start | bytes 9220 | tf_op jit(solution)/shard_map/while
  466.8 9.4 %collective-permute-start.16 = (f32[3,3,256]{0,2,1:T(8,128)S(1)}, f32[3,3,256]{0,2,1:T(8,128)S(1)}, u32[]{:S(2)}, u32[]{:S(2)}) collective-permute-start(f32[3,3,256]{0,2,1:T(8,128)S(1)} %get-tuple-element.345), channel_id=1, source_target_pairs={{0,7},{1,0},{2,1},{3,2},{4,3},{5,4},{6,5},{7,6},{8,15},{9,8},{10,9... | collective-permute-start | bytes 27656 | tf_op jit(solution)/shard_map/ppermute | solution.py:15
  466.8 9.3 %collective-permute-start.17 = (f32[3,3,256]{0,2,1:T(8,128)S(1)}, f32[3,3,256]{0,2,1:T(8,128)S(1)}, u32[]{:S(2)}, u32[]{:S(2)}) collective-permute-start(f32[3,3,256]{0,2,1:T(8,128)S(1)} %get-tuple-element.346), channel_id=1, source_target_pairs={{0,1},{1,2},{2,3},{3,4},{4,5},{5,6},{6,7},{7,0},{8,9},{9,10},{10,1... | collective-permute-start | bytes 27656 | tf_op jit(solution)/shard_map/ppermute | solution.py:15
  476.3 6.4 %collective-permute-start.18 = (f32[3,256]{0,1:T(8,128)S(1)}, f32[3,256]{0,1:T(8,128)S(1)}, u32[]{:S(2)}, u32[]{:S(2)}) collective-permute-start(f32[3,256]{0,1:T(8,128)S(1)} %get-tuple-element.347), channel_id=1, source_target_pairs={{0,24},{8,0},{16,8},{24,16},{1,25},{9,1},{17,9},{25,17},{2,26},{10... | collective-permute-start | bytes 9224 | tf_op jit(solution)/shard_map/ppermute | solution.py:15
  476.8 8.0 %collective-permute-start.19 = (f32[3,256]{0,1:T(8,128)S(1)}, f32[3,256]{0,1:T(8,128)S(1)}, u32[]{:S(2)}, u32[]{:S(2)}) collective-permute-start(f32[3,256]{0,1:T(8,128)S(1)} %get-tuple-element.348), channel_id=1, source_target_pairs={{0,8},{8,16},{16,24},{24,0},{1,9},{9,17},{17,25},{25,1},{2,10},{10... | collective-permute-start | bytes 9224 | tf_op jit(solution)/shard_map/ppermute | solution.py:15
  (138 other events, 723.4 us)
where the time goes:
time: 491 us; the launch traced here: 488 us
  other arithmetic  198 us (40%)
  local copies, waits for them, and re-layouts  157 us (32%)
  matrix products  61.1 us (12%)
  waiting for transfers between devices  47.9 us (10%)
  starting transfers between devices  18.9 us (4%)
    broadcast_in_dim x4, other arithmetic, block_energy(): jnp.sum(weighted[k][:, :, None] * carried, axis=1)  81.5 us
    scatter-add x2, other arithmetic, block_energy(): jnp.take(positions, flat_index, axis=1).reshape(3, block_rows, slots_per)  46 us
    gather x2, local copies, waits for them, and re-layouts, block_energy(): jnp.take(target_table, flat_index, axis=0)  29.8 us
    ppermute x12, waiting for transfers between devices, from_behind(): return lax.ppermute(value, axis, pairs)  26.8 us
    gather x4, local copies, waits for them, and re-layouts, block_energy(): jnp.take(positions, flat_index, axis=1).reshape(3, block_rows, slots_per)  26.4 us
    dot_general x8, matrix products, block_energy(): jnp.dot(coupled, coupler, preferred_element_type=jnp.float32)  23.4 us
    dot_general x4, matrix products, block_energy(): jnp.einsum('rnb,bc->rnc', bessel, radial_weight, precision=lax.Precision....  18.8 us
    convert_element_type x4, other arithmetic, block_energy(): (coupled * norm_scale).reshape(block_rows * slots_per, breadth)  12.3 us
  transfers between devices with their start and end apart: 20, of which 16 were waited for; matrix products, arithmetic and copies ran while one was open for 3% of the time, Pallas kernels for 0%

commit v1 on v0

--- a/solution.py
+++ b/solution.py
@@ -1,8 +1,11 @@
+import functools
 import math
 
 import jax
 import jax.numpy as jnp
 from jax import lax
+from jax.experimental import pallas as pl
+from jax.experimental.pallas import tpu as pltpu
 from jax.sharding import PartitionSpec as P
 
 soften = 0.25
@@ -28,90 +31,332 @@
     return shard
 
 
-def block_energy(
-    positions,
-    first_row,
-    neighbour_block,
-    source_block,
-    target_table,
-    radial_weight,
-    layers,
-    readout,
+def split_three(value):
+    top = value.astype(jnp.bfloat16).astype(jnp.float32)
+    rest = value - top
+    middle = rest.astype(jnp.bfloat16).astype(jnp.float32)
+    return (top, middle, rest - middle)
+
+
+def sigmoid(value):
+    return 0.5 * jnp.tanh(0.5 * value) + 0.5
+
+
+def turned(weight):
+    return weight.astype(jnp.float32).T.astype(jnp.bfloat16)
+
+
+def edge_kernel(
+    block_atoms,
+    index_smem,
+    index_ref,
+    table_ref,
+    source_ref,
+    place_ref,
+    own_ref,
+    radial_ref,
+    environ_first,
+    mixing_first,
+    coupler_first,
+    environ_second,
+    mixing_second,
+    coupler_second,
+    readout_ref,
+    scatter_ref,
+    atom_ref,
+    gathered,
+    scalars,
+    results,
+    saved,
+    forward_weights,
+    backward_weights,
+    environ_turned,
+    radial_in,
+    radial_out,
+    pick_weights,
+    place_split,
 ):
-    block_rows, slots_per = neighbour_block.shape
-    breadth = target_table.shape[1]
-    flat_index = neighbour_block.reshape(block_rows * slots_per)
-    pos_own = lax.dynamic_slice_in_dim(positions, first_row, block_rows, 1)
-    pos_far = jnp.take(positions, flat_index, axis=1).reshape(3, block_rows, slots_per)
-    offset = pos_far - pos_own[:, :, None]
-    length = jnp.sqrt(jnp.sum(offset * offset, axis=0) + soften)
-    direction = offset / length[None]
-    scaled = length / cutoff
-    smooth = (1.0 - scaled * scaled) ** 2
-    frequency = (jnp.arange(radial_weight.shape[0]) + 1).astype(jnp.float32) * math.pi
-    bessel = jnp.sin(scaled[:, :, None] * frequency) / length[:, :, None] * smooth[:, :, None]
-    radial = jnp.einsum("rnb,bc->rnc", bessel, radial_weight, precision=lax.Precision.HIGHEST)
-    gathered = jnp.take(target_table, flat_index, axis=0).reshape(block_rows, slots_per, breadth)
-    paired = source_block.astype(jnp.float32)[:, None, :] + gathered.astype(jnp.float32) + radial
-    hidden = jax.nn.silu(paired).reshape(block_rows * slots_per, breadth).astype(jnp.bfloat16)
-    weighted = direction * smooth[None]
+    slots_per, _, atom_count = index_ref.shape
+    breadth = table_ref.shape[1]
+    groups = place_ref.shape[1]
+    f32 = jnp.float32
+    bf16 = jnp.bfloat16
+    step = 16
+
+    @pl.loop(0, slots_per)
+    def _(slot):
+        @pl.loop(0, atom_count // step)
+        def _(part):
+            base = pl.multiple_of(part * step, step)
+            for u in range(step):
+                row = index_smem[slot * atom_count + base + u]
+                gathered[slot, pl.ds(base + u, 1), :] = table_ref[pl.ds(row, 1), :]
+
+    forward_weights[0, :, :breadth] = environ_first[...]
+    forward_weights[0, :, breadth:] = mixing_first[...]
+    forward_weights[1, :, :breadth] = environ_second[...]
+    forward_weights[1, :, breadth:] = mixing_second[...]
+    backward_weights[0, :, :breadth] = turned(coupler_first[...])
+    backward_weights[0, :, breadth:] = turned(mixing_first[...])
+    backward_weights[1, :, :breadth] = turned(coupler_second[...])
+    backward_weights[1, :, breadth:] = turned(mixing_second[...])
+    environ_turned[0] = turned(environ_first[...])
+    environ_turned[1] = turned(environ_second[...])
+    w_top, w_mid, w_low = split_three(radial_ref[...])
+    basis = radial_ref.shape[0]
+    lead = jnp.zeros((8, breadth), f32)
+    tail = jnp.zeros((breadth - 8 - 6 * basis, breadth), f32)
+    radial_in[...] = jnp.concatenate(
+        [lead, w_top, w_mid, w_low, w_top, w_mid, w_top, tail], axis=0
+    ).astype(bf16)
+    wide = jnp.concatenate(
+        [lead, w_top, w_mid, jnp.zeros((breadth - 8 - 2 * basis, breadth), f32)], axis=0
+    ).T.astype(bf16)
+    radial_out[:breadth, :] = wide
+    radial_out[breadth:, :] = wide
+    lane_id = lax.broadcasted_iota(jnp.int32, (breadth, breadth), 1)
+    for k in range(4):
+        pick_weights[k * breadth : (k + 1) * breadth, :] = (
+            jnp.where(lane_id == k, 1.0, 0.0).astype(bf16)
+        )
+    places = place_ref[...].reshape(3 * groups, breadth)
+    p_top, p_mid, p_low = split_three(places)
+    place_split[...] = jnp.concatenate([p_top, p_mid, p_low], axis=0).astype(bf16)
+
+    def chosen(slot):
+        index = index_ref[slot]
+        low = lax.rem(index, breadth)
+        high = lax.div(index, breadth)
+        rows = lax.broadcasted_iota(jnp.int32, (breadth, atom_count), 0)
+        one_hot = jnp.where(rows == low, 1.0, 0.0).astype(bf16)
+        group_rows = lax.broadcasted_iota(jnp.int32, (groups, atom_count), 0)
+        return (one_hot, group_rows == high)
+
+    @pl.loop(0, slots_per)
+    def _(slot):
+        one_hot, in_group = chosen(slot)
+        found = jnp.dot(place_split[...], one_hot, preferred_element_type=f32)
+        size = 3 * groups
+        found = found[:size] + found[size : 2 * size] + found[2 * size :]
+        offsets = []
+        for k in range(3):
+            far = jnp.sum(
+                jnp.where(in_group, found[k * groups : (k + 1) * groups], 0.0),
+                axis=0,
+                keepdims=True,
+            )
+            offsets.append(far - own_ref[k : k + 1, :])
+        square = offsets[0] * offsets[0] + offsets[1] * offsets[1] + offsets[2] * offsets[2]
+        length = jnp.sqrt(square + soften)
+        inverse = 1.0 / length
+        scaled = length / cutoff
+        smooth = (1.0 - scaled * scaled) ** 2
+        angle = scaled * math.pi
+        sine = jnp.sin(angle)
+        cosine = jnp.cos(angle)
+        factor = inverse * smooth
+        before, now = (jnp.zeros_like(sine), sine)
+        waves = []
+        for _ in range(basis):
+            waves.append(now * factor)
+            before, now = (now, 2.0 * cosine * now - before)
+        bessel = jnp.concatenate(waves, axis=0)
+        b_top, b_mid, b_low = split_three(bessel)
+        blank = jnp.zeros_like(sine)
+        head = [offsets[k] * inverse for k in range(3)] + [smooth] + [blank] * 4
+        spare = jnp.zeros((breadth - 8 - 6 * basis, atom_count), f32)
+        stack = jnp.concatenate(
+            head + [b_top, b_top, b_top, b_mid, b_mid, b_low, spare], axis=0
+        )
+        scalars[slot] = stack.T
+        saved[slot] = jnp.concatenate(offsets + [length, sine, cosine, blank, blank], axis=0)
+
     norm_scale = 1.0 / math.sqrt(slots_per)
-    latent = None
-    for environ, mixing, coupler in layers:
-        carried = jnp.dot(hidden, environ, preferred_element_type=jnp.float32).reshape(
-            block_rows, slots_per, breadth
+    edges = slots_per * block_atoms
+    cube = (slots_per, block_atoms, breadth)
+    readout_row = readout_ref[...].astype(f32)[None]
+    couplers = (coupler_first, coupler_second)
+    ee_lane = lax.broadcasted_iota(jnp.int32, (edges, breadth), 1) == 4
+
+    def product(left, right):
+        return jnp.dot(left.astype(bf16), right, preferred_element_type=f32)
+
+    @pl.loop(0, atom_count // block_atoms)
+    def _(block):
+        first = pl.multiple_of(block * block_atoms, block_atoms)
+        atoms = pl.ds(first, block_atoms)
+        narrow = scalars[:, atoms, :]
+        radial = product(narrow.reshape(edges, breadth), radial_in[...]).reshape(cube)
+        paired = gathered[:, atoms, :] + source_ref[atoms, :][None] + radial
+        gate = sigmoid(paired)
+        value = paired * gate
+        slopes = [gate + value * (1.0 - gate)]
+        hidden = value.reshape(edges, breadth).astype(bf16)
+        direction = [jnp.broadcast_to(narrow[:, :, k : k + 1], cube) for k in range(3)]
+        smooth = jnp.broadcast_to(narrow[:, :, 3:4], cube)
+        kept = []
+        for layer in range(2):
+            both = jnp.dot(hidden, forward_weights[layer], preferred_element_type=f32)
+            carried = both[:, :breadth].reshape(cube)
+            eased = smooth * carried
+            environment = [
+                jnp.sum(direction[k] * eased, axis=0) * norm_scale for k in range(3)
+            ]
+            coupled = direction[0] * environment[0][None]
+            coupled = coupled + direction[1] * environment[1][None]
+            coupled = coupled + direction[2] * environment[2][None]
+            mixed = both[:, breadth:] + product(
+                coupled.reshape(edges, breadth), couplers[layer][...]
+            )
+            mixed = mixed.reshape(cube)
+            gate = sigmoid(mixed)
+            value = mixed * gate
+            slopes.append(gate + value * (1.0 - gate))
+            kept.append((carried, eased, environment))
+            if layer == 0:
+                hidden = value.reshape(edges, breadth).astype(bf16)
+        edge_energy = jnp.sum(value * readout_row, axis=2, keepdims=True)
+        flow = smooth * readout_row
+        sums = None
+        for layer in (1, 0):
+            carried, eased, environment = kept[layer]
+            mixed_grad = flow * slopes[layer + 1]
+            back = product(mixed_grad.reshape(edges, breadth), backward_weights[layer])
+            coupled_grad = back[:, :breadth].reshape(cube)
+            environment_grad = [
+                jnp.sum(direction[k] * coupled_grad, axis=0) * norm_scale for k in range(3)
+            ]
+            spread = direction[0] * environment_grad[0][None]
+            spread = spread + direction[1] * environment_grad[1][None]
+            spread = spread + direction[2] * environment_grad[2][None]
+            parts = [
+                coupled_grad * environment[k][None] + eased * environment_grad[k][None]
+                for k in range(3)
+            ] + [carried * spread]
+            sums = parts if sums is None else [x + y for x, y in zip(sums, parts)]
+            flow = back[:, breadth:].reshape(cube) + product(
+                (smooth * spread).reshape(edges, breadth), environ_turned[layer]
+            ).reshape(cube)
+        paired_grad = (flow * slopes[0]).reshape(edges, breadth)
+        high = paired_grad.astype(bf16)
+        low = (paired_grad - high.astype(f32)).astype(bf16)
+        total = jnp.dot(
+            jnp.concatenate([high, low], axis=1), radial_out[...], preferred_element_type=f32
         )
-        environment = [jnp.sum(weighted[k][:, :, None] * carried, axis=1) for k in range(3)]
-        coupled = direction[0][:, :, None] * environment[0][:, None, :]
-        coupled = coupled + direction[1][:, :, None] * environment[1][:, None, :]
-        coupled = coupled + direction[2][:, :, None] * environment[2][:, None, :]
-        coupled = (
-            (coupled * norm_scale).reshape(block_rows * slots_per, breadth).astype(jnp.bfloat16)
+        total = total + jnp.dot(
+            jnp.concatenate([x.reshape(edges, breadth).astype(bf16) for x in sums], axis=1),
+            pick_weights[...],
+            preferred_element_type=f32,
         )
-        mixed = jnp.dot(hidden, mixing, preferred_element_type=jnp.float32) + jnp.dot(
-            coupled, coupler, preferred_element_type=jnp.float32
+        total = jnp.where(
+            ee_lane, jnp.broadcast_to(edge_energy, cube).reshape(edges, breadth), total
         )
-        latent = jax.nn.silu(mixed)
-        hidden = latent.astype(jnp.bfloat16)
-    edge_energy = (
-        jnp.sum(latent * readout.astype(jnp.float32)[None, :], axis=1).reshape(
-            block_rows, slots_per
-        )
-        * smooth
-    )
-    atom_energy = jnp.sum(edge_energy, axis=1)
-    return (jnp.sum(atom_energy), atom_energy)
+        results[:, atoms, :] = total.reshape(cube)
+
+    scatter_ref[...] = jnp.zeros(scatter_ref.shape, f32)
+    atom_ref[...] = jnp.zeros(atom_ref.shape, f32)
+
+    @pl.loop(0, slots_per)
+    def _(slot):
+        flat = results[slot].T
+        data = saved[slot]
+        offsets = [data[k : k + 1] for k in range(3)]
+        length, sine, cosine = (data[3:4], data[4:5], data[5:6])
+        inverse = 1.0 / length
+        scaled = length / cutoff
+        under = 1.0 - scaled * scaled
+        smooth = under * under
+        direction = [offsets[k] * inverse for k in range(3)]
+        sin_before, sin_now = (jnp.zeros_like(sine), sine)
+        cos_before, cos_now = (jnp.ones_like(sine), cosine)
+        first_sum = jnp.zeros_like(sine)
+        second_sum = jnp.zeros_like(sine)
+        for b in range(basis):
+            grad = flat[8 + b : 9 + b] + flat[8 + basis + b : 9 + basis + b]
+            first_sum = first_sum + grad * sin_now
+            second_sum = second_sum + grad * (cos_now * ((b + 1) * math.pi / cutoff))
+            sin_before, sin_now = (sin_now, 2.0 * cosine * sin_now - sin_before)
+            cos_before, cos_now = (cos_now, 2.0 * cosine * cos_now - cos_before)
+        edge_energy = flat[4:5]
+        smooth_grad = flat[3:4] + edge_energy + first_sum * inverse
+        along = flat[0:1] * direction[0] + flat[1:2] * direction[1] + flat[2:3] * direction[2]
+        length_grad = smooth * inverse * (second_sum - first_sum * inverse)
+        length_grad = length_grad - smooth_grad * under * (2.0 * scaled / cutoff) * 2.0
+        length_grad = length_grad - along * inverse
+        one_hot, in_group = chosen(slot)
+        pieces = []
+        atom_rows = []
+        for k in range(3):
+            grad = flat[k : k + 1] * inverse + length_grad * direction[k]
+            atom_rows.append(-grad)
+            pieces.append(jnp.where(in_group, jnp.broadcast_to(grad, in_group.shape), 0.0))
+        spread = jnp.concatenate(pieces, axis=0)
+        top = spread.astype(bf16)
+        low = (spread - top.astype(f32)).astype(bf16)
+        for piece in (top, low):
+            scatter_ref[...] += lax.dot_general(
+                piece, one_hot, (((1,), (1,)), ((), ())), preferred_element_type=f32
+            )
+        blank = jnp.zeros_like(sine)
+        atom_rows = atom_rows + [edge_energy * smooth] + [blank] * 4
+        atom_ref[...] += jnp.concatenate(atom_rows, axis=0)
 
 
 def device_forces(positions, neighbours, source_rows, target_table, radial_weight, layers, readout):
-    atom_count = neighbours.shape[0]
-    block_atoms = math.gcd(atom_count, 256)
-    block_count = atom_count // block_atoms
-
-    def advance(total, block_number):
-        first_row = block_number * block_atoms
-        neighbour_block = lax.dynamic_slice_in_dim(neighbours, first_row, block_atoms, 0)
-        source_block = lax.dynamic_slice_in_dim(source_rows, first_row, block_atoms, 0)
-
-        def energy_of(table_pos):
-            return block_energy(
-                table_pos,
-                first_row,
-                neighbour_block,
-                source_block,
-                target_table,
-                radial_weight,
-                layers,
-                readout,
-            )
-
-        gradient, atom_energy = jax.grad(energy_of, has_aux=True)(positions)
-        return (total + gradient, atom_energy)
-
-    total, energies = lax.scan(
-        advance, jnp.zeros(positions.shape, jnp.float32), jnp.arange(block_count, dtype=jnp.int32)
-    )
-    return (total, energies.reshape(atom_count))
+    atom_count, slots_per = neighbours.shape
+    total_rows, breadth = target_table.shape
+    basis = radial_weight.shape[0]
+    groups = -(-total_rows // breadth)
+    groups = -(-groups // 8) * 8
+    by_slot = neighbours.T
+    places = jnp.pad(positions, ((0, 0), (0, groups * breadth - total_rows)))
+    places = places.reshape(3, groups, breadth)
+    own = jnp.pad(positions[:, :atom_count], ((0, 5), (0, 0)))
+    weights = [w for layer in layers for w in layer]
+    f32 = jnp.float32
+    bf16 = jnp.bfloat16
+    vmem = pl.BlockSpec(memory_space=pltpu.VMEM)
+    smem = pl.BlockSpec(memory_space=pltpu.SMEM)
+    block_atoms = math.gcd(atom_count, 16)
+    cube = (slots_per, atom_count, breadth)
+    scattered, by_atom = pl.pallas_call(
+        functools.partial(edge_kernel, block_atoms),
+        out_shape=(
+            jax.ShapeDtypeStruct((3 * groups, breadth), f32),
+            jax.ShapeDtypeStruct((8, atom_count), f32),
+        ),
+        in_specs=[smem] + [vmem] * 13,
+        out_specs=(vmem, vmem),
+        scratch_shapes=[
+            pltpu.VMEM(cube, f32),
+            pltpu.VMEM(cube, f32),
+            pltpu.VMEM(cube, f32),
+            pltpu.VMEM((slots_per, 8, atom_count), f32),
+            pltpu.VMEM((2, breadth, 2 * breadth), bf16),
+            pltpu.VMEM((2, breadth, 2 * breadth), bf16),
+            pltpu.VMEM((2, breadth, breadth), bf16),
+            pltpu.VMEM((breadth, breadth), bf16),
+            pltpu.VMEM((2 * breadth, breadth), bf16),
+            pltpu.VMEM((4 * breadth, breadth), bf16),
+            pltpu.VMEM((9 * groups, breadth), bf16),
+        ],
+        compiler_params=pltpu.CompilerParams(vmem_limit_bytes=48 * 1024 * 1024),
+        name="edges",
+    )(
+        by_slot.reshape(-1),
+        by_slot[:, None, :],
+        target_table.astype(f32),
+        source_rows.astype(f32),
+        places,
+        own,
+        radial_weight,
+        *weights,
+        readout[None],
+    )
+    gradient = scattered.reshape(3, groups * breadth)[:, :total_rows]
+    own_part = gradient[:, :atom_count] + by_atom[:3]
+    gradient = jnp.concatenate([own_part, gradient[:, atom_count:]], axis=1)
+    return (gradient, by_atom[3])
 
 
 def move_along_x(own_rows, own_coords, slots):

time: 491 us -> 172 us (0.35)
  other arithmetic: 198 us -> 4.51 us
  local copies, waits for them, and re-layouts: 157 us -> 17 us
  Pallas kernels: 0 us -> 79.7 us
  matrix products: 61.1 us -> 0.5 us
  starting transfers between devices: 18.9 us -> 25.5 us
  waiting for transfers between devices: 47.9 us -> 42.9 us
    broadcast_in_dim x5 -> x0, other arithmetic: 81.5 us -> none  [the longest x4 81.5 us: block_energy(): jnp.sum(weighted[k][:, :, None] * carried, axis=1)]
    pallas_call x0 -> x1, Pallas kernels: none -> 79.7 us  [device_forces(): pl.pallas_call(functools.partial(edge_kernel, block_atoms), out_shape=(ja...]
    dot_general x28 -> x0, matrix products: 60.6 us -> none  [the longest x8 23.4 us: block_energy(): jnp.dot(coupled, coupler, preferred_element_type=jnp.float32)]
    gather x6 -> x0, local copies, waits for them, and re-layouts: 56.2 us -> none  [the longest x2 29.8 us: block_energy(): jnp.take(target_table, flat_index, axis=0)]
    scatter-add x2 -> x0, other arithmetic: 46 us -> none  [block_energy(): jnp.take(positions, flat_index, axis=1).reshape(3, block_rows, slots_per)]
    mul x30 -> x0, local copies, waits for them, and re-layouts: 28.9 us -> none  [the longest x8 8.24 us: block_energy(): coupled = coupled + direction[1][:, :, None] * environment[1][:, None, :]]
    reduce_sum x20 -> x0, other arithmetic: 23.7 us -> none  [the longest x4 8.79 us: block_energy(): weighted[k][:, :, None] * carried]
    convert_element_type x8 -> x0, other arithmetic: 14.8 us -> none  [the longest x4 12.3 us: block_energy(): (coupled * norm_scale).reshape(block_rows * slots_per, breadth)]
  transfers between devices with their start and end apart: 20 -> 20, of which waited for: 16 -> 14; matrix products, arithmetic and copies ran while one was open for 3% -> 7% of each run, Pallas kernels for 0% -> 0%
where the time goes in v1:
time: 172 us; the launch traced here: 171 us
  Pallas kernels  79.7 us (46%)
  waiting for transfers between devices  42.9 us (25%)
  starting transfers between devices  25.5 us (15%)
  local copies, waits for them, and re-layouts  17 us (10%)
  other arithmetic  4.51 us (3%)
    pallas_call x1, Pallas kernels, device_forces(): pl.pallas_call(functools.partial(edge_kernel, block_atoms), out_shape=(ja...  79.7 us
    ppermute x12, waiting for transfers between devices, from_behind(): return lax.ppermute(value, axis, pairs)  24.7 us
    ppermute x4, waiting for transfers between devices, extended(): before = lax.ppermute(last, axis, up)  16 us
    ppermute x12, starting transfers between devices, from_behind(): return lax.ppermute(value, axis, pairs)  12.3 us
    ppermute x4, starting transfers between devices, extended(): after = lax.ppermute(first, axis, down)  8.76 us
    ppermute x4, starting transfers between devices, extended(): before = lax.ppermute(last, axis, up)  4.36 us
  transfers between devices with their start and end apart: 20, of which 14 were waited for; matrix products, arithmetic and copies ran while one was open for 7% of the time, Pallas kernels for 0%

profile of v1, /device:TPU:0, one launch (start us, length us, event | category | flops | bytes accessed | tf_op | source)
XLA Modules:
  0.0 171.3 jit_solution(3436107371012524303)
XLA Ops:
  3.7 3.0 %collective-permute-start.8 = (f32[3,32]{0,1:T(8,128)S(1)}, f32[3,32]{0,1:T(8,128)S(1)}, u32[]{:S(2)}, u32[]{:S(2)}) collective-permute-start(f32[3,32]{0,1:T(8,128)S(1)} %bitcast.107), channel_id=1, source_target_pairs={{0,8},{8,16},{16,24},{24,0},{1,9},{9,17},{17,25},{25,1},{2,10},{10... | collective-permute-start | bytes 1160 | tf_op jit(solution)/shard_map/ppermute | solution.py:18
  7.4 1.5 collective-permute-start
  11.7 1.5 collective-permute-start.9
  13.2 2.3 %collective-permute-done.9 = f32[3,32]{0,1:T(8,128)S(1)} collective-permute-done((f32[3,32]{0,1:T(8,128)S(1)}, f32[3,32]{0,1:T(8,128)S(1)}, u32[]{:S(2)}, u32[]{:S(2)}) %collective-permute-start.9) | collective-permute-done | bytes 416 | tf_op jit(solution)/shard_map/ppermute | solution.py:18
  17.0 4.9 %collective-permute-done.10 = f32[3,32]{0,1:T(8,128)S(1)} collective-permute-done((f32[3,32]{0,1:T(8,128)S(1)}, f32[3,32]{0,1:T(8,128)S(1)}, u32[]{:S(2)}, u32[]{:S(2)}) %collective-permute-start.10) | collective-permute-done | bytes 416 | tf_op jit(solution)/shard_map/ppermute | solution.py:18
  23.3 1.4 collective-permute-done.11
  26.3 2.4 %collective-permute-start.12 = (f32[1,1,3,256]{2,3,1,0:T(8,128)S(1)}, f32[1,1,3,256]{2,3,1,0:T(8,128)S(1)}, u32[]{:S(2)}, u32[]{:S(2)}) collective-permute-start(f32[1,1,3,256]{2,3,1,0:T(8,128)S(1)} %bitcast.100), channel_id=1, source_target_pairs={{0,8},{8,16},{16,24},{24,0},{1,9},{9,17},{17,25},{25,1},{2,10},{10... | collective-permute-start | bytes 9224 | tf_op jit(solution)/shard_map/ppermute | solution.py:28
  30.6 1.5 collective-permute-start.1
  32.1 1.5 collective-permute-done.12
  33.6 1.6 collective-permute-done.13
  35.3 3.5 %collective-permute-start.15 = (f32[3,1,3,256]{2,3,1,0:T(8,128)S(1)}, f32[3,1,3,256]{2,3,1,0:T(8,128)S(1)}, u32[]{:S(2)}, u32[]{:S(2)}) collective-permute-start(f32[3,1,3,256]{2,3,1,0:T(8,128)S(1)} %pad_maximum_fusion.1), channel_id=1, source_target_pairs={{1,0},{2,1},{3,2},{4,3},{5,4},{6,5},{7,6},{0,7},{9,8},{10,9},{11,1... | collective-permute-start | bytes 27656 | tf_op jit(solution)/shard_map/ppermute | solution.py:29
  40.6 7.7 %collective-permute-done.14 = f32[3,1,3,256]{2,3,1,0:T(8,128)S(1)} collective-permute-done((f32[3,1,3,256]{2,3,1,0:T(8,128)S(1)}, f32[3,1,3,256]{2,3,1,0:T(8,128)S(1)}, u32[]{:S(2)}, u32[]{:S(2)}) %collective-permute-start.14) | collective-permute-done | bytes 9248 | tf_op jit(solution)/shard_map/ppermute | solution.py:28
  53.0 1.8 %collective-permute-start.4 = (bf16[1,1,256,128]{3,2,1,0:T(8,128)(2,1)S(1)}, bf16[1,1,256,128]{3,2,1,0:T(8,128)(2,1)S(1)}, u32[]{:S(2)}, u32[]{:S(2)}) collective-permute-start(bf16[1,1,256,128]{3,2,1,0:T(8,128)(2,1)S(1)} %bitcast.93), channel_id=1, source_target_pairs={{0,8},{8,16},{16,24},{24,0},{1,9},{9,17},{17,25},{25,1},{2,10},{10... | collective-permute-start | bytes 196616 | tf_op jit(solution)/shard_map/ppermute | solution.py:28
  56.0 2.4 %collective-permute-done.4 = bf16[1,1,256,128]{3,2,1,0:T(8,128)(2,1)S(1)} collective-permute-done((bf16[1,1,256,128]{3,2,1,0:T(8,128)(2,1)S(1)}, bf16[1,1,256,128]{3,2,1,0:T(8,128)(2,1)S(1)}, u32[]{:S(2)}, u32[]{:S(2)}) %collective-permute-start.4) | collective-permute-done | bytes 65568 | tf_op jit(solution)/shard_map/ppermute | solution.py:28
  59.2 3.5 %collective-permute-start.7 = (bf16[3,1,256,128]{3,2,1,0:T(8,128)(2,1)S(1)}, bf16[3,1,256,128]{3,2,1,0:T(8,128)(2,1)S(1)}, u32[]{:S(2)}, u32[]{:S(2)}) collective-permute-start(bf16[3,1,256,128]{3,2,1,0:T(8,128)(2,1)S(1)} %pad_maximum_fusion.2), channel_id=1, source_target_pairs={{1,0},{2,1},{3,2},{4,3},{5,4},{6,5},{7,6},{0,7},{9,8},{10,9},{11,1... | collective-permute-start | bytes 589832 | tf_op jit(solution)/shard_map/ppermute | solution.py:29
  63.0 4.5 %collective-permute-done.6 = bf16[3,1,256,128]{3,2,1,0:T(8,128)(2,1)S(1)} collective-permute-done((bf16[3,1,256,128]{3,2,1,0:T(8,128)(2,1)S(1)}, bf16[3,1,256,128]{3,2,1,0:T(8,128)(2,1)S(1)}, u32[]{:S(2)}, u32[]{:S(2)}) %collective-permute-start.6) | collective-permute-done | bytes 196640 | tf_op jit(solution)/shard_map/ppermute | solution.py:28
  68.0 79.7 %edges.1 = (f32[72,128]{1,0:T(8,128)S(1)}, f32[8,512]{1,0:T(8,128)S(1)}) custom-call(s32[8192]{0:T(1024)S(1)} %bitcast.86, s32[16,1,512]{2,1,0:T(1,128)S(1)} %broadcast_in_dim.10.index_ref, f32[2816,128]{1,0:T(8,128)S(1)} %fusion.table_ref, f32[512,128]{1,0:T(8,128)S(1)} %fusion.1.source_ref, f32[3,24,128]{2,1,0:T(8,128)S(1)} %bitcast.85, ...), custom_call_target="tpu_custom_call" | custom-call | tf_op jit(solution)/shard_map/edges/pallas_call | solution.py:322
  148.0 2.2 %collective-permute-start.16 = (f32[3,3,256]{0,2,1:T(8,128)S(1)}, f32[3,3,256]{0,2,1:T(8,128)S(1)}, u32[]{:S(2)}, u32[]{:S(2)}) collective-permute-start(f32[3,3,256]{0,2,1:T(8,128)S(1)} %bitcast.97), channel_id=1, source_target_pairs={{0,7},{1,0},{2,1},{3,2},{4,3},{5,4},{6,5},{7,6},{8,15},{9,8},{10,9... | collective-permute-start | bytes 27656 | tf_op jit(solution)/shard_map/ppermute | solution.py:18
  150.7 7.0 %collective-permute-done.16 = f32[3,3,256]{0,2,1:T(8,128)S(1)} collective-permute-done((f32[3,3,256]{0,2,1:T(8,128)S(1)}, f32[3,3,256]{0,2,1:T(8,128)S(1)}, u32[]{:S(2)}, u32[]{:S(2)}) %collective-permute-start.16) | collective-permute-done | bytes 9248 | tf_op jit(solution)/shard_map/ppermute | solution.py:18
  157.7 2.5 %collective-permute-done.17 = f32[3,3,256]{0,2,1:T(8,128)S(1)} collective-permute-done((f32[3,3,256]{0,2,1:T(8,128)S(1)}, f32[3,3,256]{0,2,1:T(8,128)S(1)}, u32[]{:S(2)}, u32[]{:S(2)}) %collective-permute-start.17) | collective-permute-done | bytes 9248 | tf_op jit(solution)/shard_map/ppermute | solution.py:18
  160.3 2.3 %collective-permute-start.18 = (f32[3,256]{0,1:T(8,128)S(1)}, f32[3,256]{0,1:T(8,128)S(1)}, u32[]{:S(2)}, u32[]{:S(2)}) collective-permute-start(f32[3,256]{0,1:T(8,128)S(1)} %get-tuple-element.14), channel_id=1, source_target_pairs={{0,24},{8,0},{16,8},{24,16},{1,25},{9,1},{17,9},{25,17},{2,26},{10... | collective-permute-start | bytes 9224 | tf_op jit(solution)/shard_map/ppermute | solution.py:18
  163.4 1.9 %collective-permute-done.18 = f32[3,256]{0,1:T(8,128)S(1)} collective-permute-done((f32[3,256]{0,1:T(8,128)S(1)}, f32[3,256]{0,1:T(8,128)S(1)}, u32[]{:S(2)}, u32[]{:S(2)}) %collective-permute-start.18) | collective-permute-done | bytes 3104 | tf_op jit(solution)/shard_map/ppermute | solution.py:18
  165.3 3.2 %collective-permute-done.19 = f32[3,256]{0,1:T(8,128)S(1)} collective-permute-done((f32[3,256]{0,1:T(8,128)S(1)}, f32[3,256]{0,1:T(8,128)S(1)}, u32[]{:S(2)}, u32[]{:S(2)}) %collective-permute-start.19) | collective-permute-done | bytes 3104 | tf_op jit(solution)/shard_map/ppermute | solution.py:18
  168.5 2.1 %scatter_custom_fusion.8 = f32[3,512]{0,1:T(8,128)S(1)} fusion(f32[3,512]{0,1:T(8,128)S(1)} %copy.59, s32[256]{0:T(256)S(1)} %bitcast.106, f32[3,256]{0,1:T(8,128)S(1)} %collective-permute-done.19, f32[3,256]{0,1:T(8,128)S(1)} %collective-permute-done.18, f32[3,3,256]{0,2,1:T(8,128)S(1)} %fusion.5), kind=kCustom, calls=%fused_computation.38 | custom fusion | flops 2304 | bytes 399360 | tf_op jit(solution)/shard_map/scatter-add | solution.py:440
  (97 shorter events, 24.1 us)
Async XLA Ops:
  0.6 66.9 %copy-start = (bf16[128,128]{1,0:T(8,128)(2,1)S(1)}, bf16[128,128]{1,0:T(8,128)(2,1)}, u32[]{:S(2)}) copy-start(bf16[128,128]{1,0:T(8,128)(2,1)} %param.23) | copy-start | bytes 98308
  1.6 38.7 %copy-start.9 = (s32[1,1,512,16]{2,3,1,0:T(8,128)S(1)}, s32[1,1,512,16]{2,3,1,0:T(8,128)}, u32[]{:S(2)}) copy-start(s32[1,1,512,16]{2,3,1,0:T(8,128)} %param.21) | copy-start | bytes 98308
  3.7 6.6 %collective-permute-start.8 = (f32[3,32]{0,1:T(8,128)S(1)}, f32[3,32]{0,1:T(8,128)S(1)}, u32[]{:S(2)}, u32[]{:S(2)}) collective-permute-start(f32[3,32]{0,1:T(8,128)S(1)} %bitcast.107), channel_id=1, source_target_pairs={{0,8},{8,16},{16,24},{24,0},{1,9},{9,17},{17,25},{25,1},{2,10},{10... | collective-permute-start | bytes 1160 | tf_op jit(solution)/shard_map/ppermute | solution.py:18
  7.4 21.9 %collective-permute-start = (bf16[32,128]{1,0:T(8,128)(2,1)S(1)}, bf16[32,128]{1,0:T(8,128)(2,1)S(1)}, u32[]{:S(2)}, u32[]{:S(2)}) collective-permute-start(bf16[32,128]{1,0:T(8,128)(2,1)S(1)} %gather_fusion), channel_id=1, source_target_pairs={{0,8},{8,16},{16,24},{24,0},{1,9},{9,17},{17,25},{25,1},{2,10},{10... | collective-permute-start | bytes 24584 | tf_op jit(solution)/shard_map/ppermute | solution.py:18
  11.7 3.8 %collective-permute-start.9 = (f32[3,32]{0,1:T(8,128)S(1)}, f32[3,32]{0,1:T(8,128)S(1)}, u32[]{:S(2)}, u32[]{:S(2)}) collective-permute-start(f32[3,32]{0,1:T(8,128)S(1)} %bitcast.109), channel_id=1, source_target_pairs={{0,24},{8,0},{16,8},{24,16},{1,25},{9,1},{17,9},{25,17},{2,26},{10... | collective-permute-start | bytes 1160 | tf_op jit(solution)/shard_map/ppermute | solution.py:18
  16.9 5.0 %collective-permute-start.10 = (f32[3,32]{0,1:T(8,128)S(1)}, f32[3,32]{0,1:T(8,128)S(1)}, u32[]{:S(2)}, u32[]{:S(2)}) collective-permute-start(f32[3,32]{0,1:T(8,128)S(1)} %bitcast.108), channel_id=1, source_target_pairs={{0,1},{1,2},{2,3},{3,4},{4,5},{5,6},{6,7},{7,0},{8,9},{9,10},{10,1... | collective-permute-start | bytes 1160 | tf_op jit(solution)/shard_map/ppermute | solution.py:18
  23.3 1.5 collective-permute-start.11
  26.3 7.3 %collective-permute-start.12 = (f32[1,1,3,256]{2,3,1,0:T(8,128)S(1)}, f32[1,1,3,256]{2,3,1,0:T(8,128)S(1)}, u32[]{:S(2)}, u32[]{:S(2)}) collective-permute-start(f32[1,1,3,256]{2,3,1,0:T(8,128)S(1)} %bitcast.100), channel_id=1, source_target_pairs={{0,8},{8,16},{16,24},{24,0},{1,9},{9,17},{17,25},{25,1},{2,10},{10... | collective-permute-start | bytes 9224 | tf_op jit(solution)/shard_map/ppermute | solution.py:28
  28.7 6.5 %collective-permute-start.13 = (f32[1,1,3,256]{2,3,1,0:T(8,128)S(1)}, f32[1,1,3,256]{2,3,1,0:T(8,128)S(1)}, u32[]{:S(2)}, u32[]{:S(2)}) collective-permute-start(f32[1,1,3,256]{2,3,1,0:T(8,128)S(1)} %bitcast.101), channel_id=1, source_target_pairs={{8,0},{16,8},{24,16},{0,24},{9,1},{17,9},{25,17},{1,25},{10,2},{18... | collective-permute-start | bytes 9224 | tf_op jit(solution)/shard_map/ppermute | solution.py:29
  30.6 8.2 %collective-permute-start.1 = (bf16[32,128]{1,0:T(8,128)(2,1)S(1)}, bf16[32,128]{1,0:T(8,128)(2,1)S(1)}, u32[]{:S(2)}, u32[]{:S(2)}) collective-permute-start(bf16[32,128]{1,0:T(8,128)(2,1)S(1)} %gather_fusion.1), channel_id=1, source_target_pairs={{0,24},{8,0},{16,8},{24,16},{1,25},{9,1},{17,9},{25,17},{2,26},{10... | collective-permute-start | bytes 24584 | tf_op jit(solution)/shard_map/ppermute | solution.py:18
  35.2 13.0 %collective-permute-start.14 = (f32[3,1,3,256]{2,3,1,0:T(8,128)S(1)}, f32[3,1,3,256]{2,3,1,0:T(8,128)S(1)}, u32[]{:S(2)}, u32[]{:S(2)}) collective-permute-start(f32[3,1,3,256]{2,3,1,0:T(8,128)S(1)} %pad_maximum_fusion.1), channel_id=1, source_target_pairs={{0,1},{1,2},{2,3},{3,4},{4,5},{5,6},{6,7},{7,0},{8,9},{9,10},{10,1... | collective-permute-start | bytes 27656 | tf_op jit(solution)/shard_map/ppermute | solution.py:28
  35.3 13.1 %collective-permute-start.15 = (f32[3,1,3,256]{2,3,1,0:T(8,128)S(1)}, f32[3,1,3,256]{2,3,1,0:T(8,128)S(1)}, u32[]{:S(2)}, u32[]{:S(2)}) collective-permute-start(f32[3,1,3,256]{2,3,1,0:T(8,128)S(1)} %pad_maximum_fusion.1), channel_id=1, source_target_pairs={{1,0},{2,1},{3,2},{4,3},{5,4},{6,5},{7,6},{0,7},{9,8},{10,9},{11,1... | collective-permute-start | bytes 27656 | tf_op jit(solution)/shard_map/ppermute | solution.py:29
  40.2 8.4 %collective-permute-start.2 = (bf16[32,128]{1,0:T(8,128)(2,1)S(1)}, bf16[32,128]{1,0:T(8,128)(2,1)S(1)}, u32[]{:S(2)}, u32[]{:S(2)}) collective-permute-start(bf16[32,128]{1,0:T(8,128)(2,1)S(1)} %gather_fusion.2), channel_id=1, source_target_pairs={{0,1},{1,2},{2,3},{3,4},{4,5},{5,6},{6,7},{7,0},{8,9},{9,10},{10,1... | collective-permute-start | bytes 24584 | tf_op jit(solution)/shard_map/ppermute | solution.py:18
  40.4 22.3 %copy-start.10 = (bf16[128,128]{1,0:T(8,128)(2,1)S(1)}, bf16[128,128]{1,0:T(8,128)(2,1)}, u32[]{:S(2)}) copy-start(bf16[128,128]{1,0:T(8,128)(2,1)} %param.22) | copy-start | bytes 98308
  50.0 1.4 collective-permute-start.3
  53.0 5.4 %collective-permute-start.4 = (bf16[1,1,256,128]{3,2,1,0:T(8,128)(2,1)S(1)}, bf16[1,1,256,128]{3,2,1,0:T(8,128)(2,1)S(1)}, u32[]{:S(2)}, u32[]{:S(2)}) collective-permute-start(bf16[1,1,256,128]{3,2,1,0:T(8,128)(2,1)S(1)} %bitcast.93), channel_id=1, source_target_pairs={{0,8},{8,16},{16,24},{24,0},{1,9},{9,17},{17,25},{25,1},{2,10},{10... | collective-permute-start | bytes 196616 | tf_op jit(solution)/shard_map/ppermute | solution.py:28
  54.8 4.3 %collective-permute-start.5 = (bf16[1,1,256,128]{3,2,1,0:T(8,128)(2,1)S(1)}, bf16[1,1,256,128]{3,2,1,0:T(8,128)(2,1)S(1)}, u32[]{:S(2)}, u32[]{:S(2)}) collective-permute-start(bf16[1,1,256,128]{3,2,1,0:T(8,128)(2,1)S(1)} %bitcast.94), channel_id=1, source_target_pairs={{8,0},{16,8},{24,16},{0,24},{9,1},{17,9},{25,17},{1,25},{10,2},{18... | collective-permute-start | bytes 196616 | tf_op jit(solution)/shard_map/ppermute | solution.py:29
  59.1 8.3 %collective-permute-start.6 = (bf16[3,1,256,128]{3,2,1,0:T(8,128)(2,1)S(1)}, bf16[3,1,256,128]{3,2,1,0:T(8,128)(2,1)S(1)}, u32[]{:S(2)}, u32[]{:S(2)}) collective-permute-start(bf16[3,1,256,128]{3,2,1,0:T(8,128)(2,1)S(1)} %pad_maximum_fusion.2), channel_id=1, source_target_pairs={{0,1},{1,2},{2,3},{3,4},{4,5},{5,6},{6,7},{7,0},{8,9},{9,10},{10,1... | collective-permute-start | bytes 589832 | tf_op jit(solution)/shard_map/ppermute | solution.py:28
  59.2 8.3 %collective-permute-start.7 = (bf16[3,1,256,128]{3,2,1,0:T(8,128)(2,1)S(1)}, bf16[3,1,256,128]{3,2,1,0:T(8,128)(2,1)S(1)}, u32[]{:S(2)}, u32[]{:S(2)}) collective-permute-start(bf16[3,1,256,128]{3,2,1,0:T(8,128)(2,1)S(1)} %pad_maximum_fusion.2), channel_id=1, source_target_pairs={{1,0},{2,1},{3,2},{4,3},{5,4},{6,5},{7,6},{0,7},{9,8},{10,9},{11,1... | collective-permute-start | bytes 589832 | tf_op jit(solution)/shard_map/ppermute | solution.py:29
  62.9 5.0 %copy-start.1 = (bf16[128,128]{1,0:T(8,128)(2,1)S(1)}, bf16[128,128]{1,0:T(8,128)(2,1)}, u32[]{:S(2)}) copy-start(bf16[128,128]{1,0:T(8,128)(2,1)} %environ_first.1) | copy-start | bytes 98308
  148.0 9.7 %collective-permute-start.16 = (f32[3,3,256]{0,2,1:T(8,128)S(1)}, f32[3,3,256]{0,2,1:T(8,128)S(1)}, u32[]{:S(2)}, u32[]{:S(2)}) collective-permute-start(f32[3,3,256]{0,2,1:T(8,128)S(1)} %bitcast.97), channel_id=1, source_target_pairs={{0,7},{1,0},{2,1},{3,2},{4,3},{5,4},{6,5},{7,6},{8,15},{9,8},{10,9... | collective-permute-start | bytes 27656 | tf_op jit(solution)/shard_map/ppermute | solution.py:18
  150.4 9.8 %collective-permute-start.17 = (f32[3,3,256]{0,2,1:T(8,128)S(1)}, f32[3,3,256]{0,2,1:T(8,128)S(1)}, u32[]{:S(2)}, u32[]{:S(2)}) collective-permute-start(f32[3,3,256]{0,2,1:T(8,128)S(1)} %bitcast.98), channel_id=1, source_target_pairs={{0,1},{1,2},{2,3},{3,4},{4,5},{5,6},{6,7},{7,0},{8,9},{9,10},{10,1... | collective-permute-start | bytes 27656 | tf_op jit(solution)/shard_map/ppermute | solution.py:18
  160.3 5.0 %collective-permute-start.18 = (f32[3,256]{0,1:T(8,128)S(1)}, f32[3,256]{0,1:T(8,128)S(1)}, u32[]{:S(2)}, u32[]{:S(2)}) collective-permute-start(f32[3,256]{0,1:T(8,128)S(1)} %get-tuple-element.14), channel_id=1, source_target_pairs={{0,24},{8,0},{16,8},{24,16},{1,25},{9,1},{17,9},{25,17},{2,26},{10... | collective-permute-start | bytes 9224 | tf_op jit(solution)/shard_map/ppermute | solution.py:18
  162.6 5.9 %collective-permute-start.19 = (f32[3,256]{0,1:T(8,128)S(1)}, f32[3,256]{0,1:T(8,128)S(1)}, u32[]{:S(2)}, u32[]{:S(2)}) collective-permute-start(f32[3,256]{0,1:T(8,128)S(1)} %get-tuple-element.15), channel_id=1, source_target_pairs={{0,8},{8,16},{16,24},{24,0},{1,9},{9,17},{17,25},{25,1},{2,10},{10... | collective-permute-start | bytes 9224 | tf_op jit(solution)/shard_map/ppermute | solution.py:18
  (7 other events, 34.9 us)

commit v2 on v1

--- a/solution.py
+++ b/solution.py
@@ -10,25 +10,6 @@
 
 soften = 0.25
 cutoff = 2.0
-
-
-def from_behind(value, axis, steps):
-    count = lax.axis_size(axis)
-    pairs = [(source, (source + steps) % count) for source in range(count)]
-    return lax.ppermute(value, axis, pairs)
-
-
-def extended(shard, sides, width):
-    for axis, dim in sides:
-        count, length = (lax.axis_size(axis), shard.shape[dim])
-        up = [(i, (i + 1) % count) for i in range(count)]
-        down = [(j, i) for i, j in up]
-        last = lax.slice_in_dim(shard, length - width, length, axis=dim)
-        first = lax.slice_in_dim(shard, 0, width, axis=dim)
-        before = lax.ppermute(last, axis, up)
-        after = lax.ppermute(first, axis, down)
-        shard = jnp.concatenate([before, shard, after], axis=dim)
-    return shard
 
 
 def split_three(value):
@@ -302,94 +283,215 @@
         atom_ref[...] += jnp.concatenate(atom_rows, axis=0)
 
 
-def device_forces(positions, neighbours, source_rows, target_table, radial_weight, layers, readout):
-    atom_count, slots_per = neighbours.shape
-    total_rows, breadth = target_table.shape
-    basis = radial_weight.shape[0]
-    groups = -(-total_rows // breadth)
-    groups = -(-groups // 8) * 8
-    by_slot = neighbours.T
-    places = jnp.pad(positions, ((0, 0), (0, groups * breadth - total_rows)))
-    places = places.reshape(3, groups, breadth)
-    own = jnp.pad(positions[:, :atom_count], ((0, 5), (0, 0)))
-    weights = [w for layer in layers for w in layer]
+def others(shape):
+    here = (lax.axis_index("gx"), lax.axis_index("gy"))
+    steps = [(n // 3 - 1, n % 3 - 1) for n in range(9)]
+
+    def at(dx, dy):
+        return (
+            lax.rem(here[0] + (dx + shape[0]), shape[0]),
+            lax.rem(here[1] + (dy + shape[1]), shape[1]),
+        )
+
+    return (at, steps)
+
+
+def greet(shape):
+    at, steps = others(shape)
+    barrier = pltpu.get_barrier_semaphore()
+    for dx, dy in steps:
+        if (dx, dy) != (0, 0):
+            pl.semaphore_signal(
+                barrier, inc=1, device_id=at(dx, dy), device_id_type=pl.DeviceIdType.MESH
+            )
+    return barrier
+
+
+def hot_columns(slots, count):
+    rows = lax.broadcasted_iota(jnp.int32, (count, slots.shape[1]), 0)
+    return jnp.where(rows == slots, 1.0, 0.0)
+
+
+def share_kernel(
+    shape,
+    features,
+    coords,
+    slots_x,
+    slots_y,
+    ghosts,
+    source_weight,
+    target_weight,
+    table_ref,
+    source_ref,
+    place_ref,
+    own_ref,
+    holding,
+    leaving,
+    arriving,
+    ghost_rows,
+    ghost_places,
+    halo_rows,
+    halo_places,
+    move_send,
+    move_recv,
+    rows_send,
+    rows_recv,
+    places_send,
+    places_recv,
+):
     f32 = jnp.float32
     bf16 = jnp.bfloat16
-    vmem = pl.BlockSpec(memory_space=pltpu.VMEM)
-    smem = pl.BlockSpec(memory_space=pltpu.SMEM)
-    block_atoms = math.gcd(atom_count, 16)
-    cube = (slots_per, atom_count, breadth)
-    scattered, by_atom = pl.pallas_call(
-        functools.partial(edge_kernel, block_atoms),
-        out_shape=(
-            jax.ShapeDtypeStruct((3 * groups, breadth), f32),
-            jax.ShapeDtypeStruct((8, atom_count), f32),
-        ),
-        in_specs=[smem] + [vmem] * 13,
-        out_specs=(vmem, vmem),
-        scratch_shapes=[
-            pltpu.VMEM(cube, f32),
-            pltpu.VMEM(cube, f32),
-            pltpu.VMEM(cube, f32),
-            pltpu.VMEM((slots_per, 8, atom_count), f32),
-            pltpu.VMEM((2, breadth, 2 * breadth), bf16),
-            pltpu.VMEM((2, breadth, 2 * breadth), bf16),
-            pltpu.VMEM((2, breadth, breadth), bf16),
-            pltpu.VMEM((breadth, breadth), bf16),
-            pltpu.VMEM((2 * breadth, breadth), bf16),
-            pltpu.VMEM((4 * breadth, breadth), bf16),
-            pltpu.VMEM((9 * groups, breadth), bf16),
-        ],
-        compiler_params=pltpu.CompilerParams(vmem_limit_bytes=48 * 1024 * 1024),
-        name="edges",
-    )(
-        by_slot.reshape(-1),
-        by_slot[:, None, :],
-        target_table.astype(f32),
-        source_rows.astype(f32),
-        places,
-        own,
-        radial_weight,
-        *weights,
-        readout[None],
+    mesh_ids = pl.DeviceIdType.MESH
+    count, breadth = features.shape
+    sent = slots_x.shape[1] // 2
+    ghost_count = ghosts.shape[1]
+    at, steps = others(shape)
+    barrier = greet(shape)
+
+    blank = jnp.zeros((5, count), f32)
+    pieces = []
+    for piece in split_three(coords[...]):
+        pieces += [piece, blank]
+    pieces.append(jnp.zeros((breadth - 24, count), f32))
+    holding[:, :breadth] = features[...]
+    holding[:, breadth:] = jnp.concatenate(pieces, axis=0).T.astype(bf16)
+    both = jnp.concatenate([slots_x[...], slots_y[...]], axis=1)
+    picks = hot_columns(both, count).T.astype(bf16)
+    ghost_hot = hot_columns(ghosts[...], count)
+    ghost_picks = ghost_hot.T.astype(bf16)
+    ghost_hot = ghost_hot.astype(bf16)
+
+    for axis, slots in ((0, slots_x), (1, slots_y)):
+        chosen = picks[2 * sent * axis : 2 * sent * (axis + 1)]
+        payload = jnp.dot(chosen, holding[...], preferred_element_type=f32).astype(bf16)
+        leaving[axis, 0] = payload[:sent]
+        leaving[axis, 1] = payload[sent:]
+        put = hot_columns(slots[...], count)
+        hit = jnp.max(put, axis=1, keepdims=True) > 0.5
+        put = put.astype(bf16)
+        if axis == 0:
+            pl.semaphore_wait(barrier, 8)
+        copies = []
+        for way, stride in ((0, 1), (1, -1)):
+            copy = pltpu.make_async_remote_copy(
+                src_ref=leaving.at[axis, way],
+                dst_ref=arriving.at[axis, way],
+                send_sem=move_send.at[axis, way],
+                recv_sem=move_recv.at[axis, way],
+                device_id=at(stride, 0) if axis == 0 else at(0, stride),
+                device_id_type=mesh_ids,
+            )
+            copy.start()
+            copies.append(copy)
+        for copy in copies:
+            copy.wait()
+        came = arriving[axis].reshape(2 * sent, 2 * breadth)
+        moved = jnp.dot(put, came, preferred_element_type=f32)
+        holding[...] = jnp.where(hit, moved, holding[...].astype(f32)).astype(bf16)
+
+    rows = holding[:, :breadth]
+    target = jnp.dot(rows, target_weight[...], preferred_element_type=f32).astype(bf16)
+    ghost_rows[...] = jnp.dot(ghost_picks, target, preferred_element_type=f32).astype(bf16)
+    flat = holding[:, breadth:].astype(f32).T[:24]
+    ghost_flat = jnp.dot(flat.astype(bf16), ghost_hot, preferred_element_type=f32)
+    ghost_places[...] = ghost_flat[:8] + ghost_flat[8:16] + ghost_flat[16:24]
+    copies = {}
+    for n, (dx, dy) in enumerate(steps):
+        if (dx, dy) == (0, 0):
+            continue
+        copies[n] = []
+        for source, landing, send, recv in (
+            (ghost_places, halo_places, places_send, places_recv),
+            (ghost_rows, halo_rows, rows_send, rows_recv),
+        ):
+            copy = pltpu.make_async_remote_copy(
+                src_ref=source,
+                dst_ref=landing.at[n],
+                send_sem=send.at[n],
+                recv_sem=recv.at[n],
+                device_id=at(-dx, -dy),
+                device_id_type=mesh_ids,
+            )
+            copy.start()
+            copies[n].append(copy)
+    table_ref[:count, :] = target.astype(f32)
+    source_ref[...] = (
+        jnp.dot(rows, source_weight[...], preferred_element_type=f32).astype(bf16).astype(f32)
     )
-    gradient = scattered.reshape(3, groups * breadth)[:, :total_rows]
-    own_part = gradient[:, :atom_count] + by_atom[:3]
-    gradient = jnp.concatenate([own_part, gradient[:, atom_count:]], axis=1)
-    return (gradient, by_atom[3])
-
-
-def move_along_x(own_rows, own_coords, slots):
-    for column, stride in ((0, 1), (1, -1)):
-        picked = slots[column]
-        arrived_rows = from_behind(own_rows[picked], "gx", stride)
-        arrived_coords = from_behind(own_coords[:, picked], "gx", stride)
-        own_rows = own_rows.at[picked].set(arrived_rows)
-        own_coords = own_coords.at[:, picked].set(arrived_coords)
-    return (own_rows, own_coords)
-
-
-def move_along_y(own_rows, own_coords, slots):
-    for column, stride in ((0, 1), (1, -1)):
-        picked = slots[column]
-        arrived_rows = from_behind(own_rows[picked], "gy", stride)
-        arrived_coords = from_behind(own_coords[:, picked], "gy", stride)
-        own_rows = own_rows.at[picked].set(arrived_rows)
-        own_coords = own_coords.at[:, picked].set(arrived_coords)
-    return (own_rows, own_coords)
-
-
-def fold_back(ghost_grad):
-    partial_sum = ghost_grad[:, :, 1]
-    for column, stride in ((0, -1), (2, 1)):
-        partial_sum = partial_sum + from_behind(ghost_grad[:, :, column], "gy", stride)
-    whole = partial_sum[:, 1]
-    for column, stride in ((0, -1), (2, 1)):
-        whole = whole + from_behind(partial_sum[:, column], "gx", stride)
-    return whole
+    mine = flat[:8] + flat[8:16] + flat[16:24]
+    own_ref[...] = mine
+    place_ref[...] = jnp.zeros(place_ref.shape, f32)
+    own_groups = count // breadth
+    for k in range(3):
+        for g in range(own_groups):
+            place_ref[k, g : g + 1, :] = mine[k : k + 1, g * breadth : (g + 1) * breadth]
+    ghost_groups = ghost_count // breadth
+    for n in range(9):
+        rows_at = pl.ds(count + n * ghost_count, ghost_count)
+        if n not in copies:
+            table_ref[rows_at, :] = jnp.zeros((ghost_count, breadth), f32)
+            continue
+        for copy in copies[n]:
+            copy.wait()
+        table_ref[rows_at, :] = halo_rows[n].astype(f32)
+        places = halo_places[n]
+        for k in range(3):
+            for g in range(ghost_groups):
+                group = own_groups + n * ghost_groups + g
+                place_ref[k, group : group + 1, :] = places[
+                    k : k + 1, g * breadth : (g + 1) * breadth
+                ]
+
+
+def return_kernel(
+    shape, scattered, by_atom, ghosts, force_ref, leaving, arriving, send_sem, recv_sem
+):
+    f32 = jnp.float32
+    bf16 = jnp.bfloat16
+    count = by_atom.shape[1]
+    breadth = scattered.shape[2]
+    ghost_groups = ghosts.shape[1] // breadth
+    own_groups = count // breadth
+    at, steps = others(shape)
+    barrier = greet(shape)
+    blank = jnp.zeros((5, breadth), f32)
+    for n in range(9):
+        for g in range(ghost_groups):
+            group = own_groups + n * ghost_groups + g
+            piece = [scattered[k, group : group + 1, :] for k in range(3)]
+            leaving[n, :, g * breadth : (g + 1) * breadth] = jnp.concatenate(
+                piece + [blank], axis=0
+            )
+    spots = hot_columns(ghosts[...], count).T.astype(bf16)
+    pl.semaphore_wait(barrier, 8)
+    copies = []
+    for n, (dx, dy) in enumerate(steps):
+        if (dx, dy) == (0, 0):
+            continue
+        copy = pltpu.make_async_remote_copy(
+            src_ref=leaving.at[n],
+            dst_ref=arriving.at[n],
+            send_sem=send_sem.at[n],
+            recv_sem=recv_sem.at[n],
+            device_id=at(dx, dy),
+            device_id_type=pl.DeviceIdType.MESH,
+        )
+        copy.start()
+        copies.append((n, copy))
+    total = leaving[4]
+    for n, copy in copies:
+        copy.wait()
+        total = total + arriving[n]
+    stack = jnp.concatenate(split_three(total), axis=0).astype(bf16)
+    back = jnp.dot(stack, spots, preferred_element_type=f32)
+    back = back[:8] + back[8:16] + back[16:24]
+    for k in range(3):
+        own = jnp.concatenate([scattered[k, g : g + 1, :] for g in range(own_groups)], axis=1)
+        force_ref[k : k + 1, :] = -(own + by_atom[k : k + 1, :] + back[k : k + 1, :])
 
 
 def per_device(
+    shape,
     features,
     coords,
     migrate_x_slots,
@@ -407,38 +509,114 @@
     coupler_second,
     readout,
 ):
-    own_rows = features[0, 0]
-    own_coords = coords[0, 0]
-    own_rows, own_coords = move_along_x(own_rows, own_coords, migrate_x_slots[0, 0])
-    own_rows, own_coords = move_along_y(own_rows, own_coords, migrate_y_slots[0, 0])
-    atom_count = own_rows.shape[0]
-    ghosts = ghost_slots[0, 0]
-    ghost_count = ghosts.shape[0]
-    ghost_coords = own_coords[:, ghosts]
-    source_rows = jnp.dot(own_rows, source_weight, preferred_element_type=jnp.float32).astype(
-        jnp.bfloat16
+    features = features[0, 0]
+    coords = coords[0, 0]
+    neighbours = neighbours[0, 0]
+    ghosts = ghost_slots.reshape(1, -1)
+    count, breadth = features.shape
+    slots_per = neighbours.shape[1]
+    ghost_count = ghosts.shape[1]
+    sent = migrate_x_slots.shape[3]
+    total_rows = count + 9 * ghost_count
+    groups = -(-(total_rows // breadth) // 8) * 8
+    f32 = jnp.float32
+    bf16 = jnp.bfloat16
+    vmem = pl.BlockSpec(memory_space=pltpu.VMEM)
+    smem = pl.BlockSpec(memory_space=pltpu.SMEM)
+    dma = pltpu.SemaphoreType.DMA
+    table, source_rows, places, own = pl.pallas_call(
+        functools.partial(share_kernel, shape),
+        out_shape=(
+            jax.ShapeDtypeStruct((total_rows, breadth), f32),
+            jax.ShapeDtypeStruct((count, breadth), f32),
+            jax.ShapeDtypeStruct((3, groups, breadth), f32),
+            jax.ShapeDtypeStruct((8, count), f32),
+        ),
+        in_specs=[vmem] * 7,
+        out_specs=(vmem,) * 4,
+        scratch_shapes=[
+            pltpu.VMEM((count, 2 * breadth), bf16),
+            pltpu.VMEM((2, 2, sent, 2 * breadth), bf16),
+            pltpu.VMEM((2, 2, sent, 2 * breadth), bf16),
+            pltpu.VMEM((ghost_count, breadth), bf16),
+            pltpu.VMEM((8, ghost_count), f32),
+            pltpu.VMEM((9, ghost_count, breadth), bf16),
+            pltpu.VMEM((9, 8, ghost_count), f32),
+            dma((2, 2)),
+            dma((2, 2)),
+            dma((9,)),
+            dma((9,)),
+            dma((9,)),
+            dma((9,)),
+        ],
+        compiler_params=pltpu.CompilerParams(collective_id=0, has_side_effects=True),
+        name="share",
+    )(
+        features,
+        coords,
+        migrate_x_slots.reshape(1, -1),
+        migrate_y_slots.reshape(1, -1),
+        ghosts,
+        source_weight,
+        target_weight,
     )
-    payload = own_rows[ghosts]
-    breadth = payload.shape[1]
-    halo_rows = extended(payload[None, None], (("gx", 0), ("gy", 1)), 1)
-    halo_coords = extended(ghost_coords[None, None], (("gx", 0), ("gy", 1)), 1)
-    stacked = jnp.concatenate([own_rows, halo_rows.reshape(9 * ghost_count, breadth)], axis=0)
-    target_table = jnp.dot(stacked, target_weight, preferred_element_type=jnp.float32).astype(
-        jnp.bfloat16
+    by_slot = neighbours.T
+    block_atoms = math.gcd(count, 16)
+    cube = (slots_per, count, breadth)
+    scattered, by_atom = pl.pallas_call(
+        functools.partial(edge_kernel, block_atoms),
+        out_shape=(
+            jax.ShapeDtypeStruct((3 * groups, breadth), f32),
+            jax.ShapeDtypeStruct((8, count), f32),
+        ),
+        in_specs=[smem] + [vmem] * 13,
+        out_specs=(vmem, vmem),
+        scratch_shapes=[
+            pltpu.VMEM(cube, f32),
+            pltpu.VMEM(cube, f32),
+            pltpu.VMEM(cube, f32),
+            pltpu.VMEM((slots_per, 8, count), f32),
+            pltpu.VMEM((2, breadth, 2 * breadth), bf16),
+            pltpu.VMEM((2, breadth, 2 * breadth), bf16),
+            pltpu.VMEM((2, breadth, breadth), bf16),
+            pltpu.VMEM((breadth, breadth), bf16),
+            pltpu.VMEM((2 * breadth, breadth), bf16),
+            pltpu.VMEM((4 * breadth, breadth), bf16),
+            pltpu.VMEM((9 * groups, breadth), bf16),
+        ],
+        compiler_params=pltpu.CompilerParams(vmem_limit_bytes=48 * 1024 * 1024),
+        name="edges",
+    )(
+        by_slot.reshape(-1),
+        by_slot[:, None, :],
+        table,
+        source_rows,
+        places,
+        own,
+        radial_weight,
+        environ_first,
+        mixing_first,
+        coupler_first,
+        environ_second,
+        mixing_second,
+        coupler_second,
+        readout[None],
     )
-    positions = jnp.concatenate(
-        [own_coords, jnp.moveaxis(halo_coords, 2, 0).reshape(3, 9 * ghost_count)], axis=1
-    )
-    layers = (
-        (environ_first, mixing_first, coupler_first),
-        (environ_second, mixing_second, coupler_second),
-    )
-    gradient, energies = device_forces(
-        positions, neighbours[0, 0], source_rows, target_table, radial_weight, layers, readout
-    )
-    returned = fold_back(gradient[:, atom_count:].reshape(3, 3, 3, ghost_count))
-    total = gradient[:, :atom_count].at[:, ghosts].add(returned)
-    return ((-total)[None, None], energies[None, None])
+    forces = pl.pallas_call(
+        functools.partial(return_kernel, shape),
+        out_shape=jax.ShapeDtypeStruct((3, count), f32),
+        in_specs=[vmem] * 3,
+        out_specs=vmem,
+        scratch_shapes=[
+            pltpu.VMEM((9, 8, ghost_count), f32),
+            pltpu.VMEM((9, 8, ghost_count), f32),
+            dma((9,)),
+            dma((9,)),
+        ],
+        compiler_params=pltpu.CompilerParams(collective_id=1, has_side_effects=True),
+        name="give_back",
+    )(scattered.reshape(3, groups, breadth), by_atom, ghosts)
+    return (forces[None, None], by_atom[3][None, None])
 
 
 def solution(mesh):
@@ -462,5 +640,6 @@
     )
     out_specs = (P("gx", "gy", None, None), P("gx", "gy", None))
     return jax.shard_map(
-        per_device, mesh=mesh, in_specs=in_specs, out_specs=out_specs, check_vma=False
+        functools.partial(per_device, (mesh.shape["gx"], mesh.shape["gy"])),
+        mesh=mesh, in_specs=in_specs, out_specs=out_specs, check_vma=False
     )

time: 172 us -> 134 us (0.78)
  waiting for transfers between devices: 42.9 us -> 0 us
  Pallas kernels: 79.7 us -> 114 us
  starting transfers between devices: 25.5 us -> 0 us
  other arithmetic: 4.51 us -> 0 us
  local copies, waits for them, and re-layouts: 17 us -> 18.8 us
    ppermute x20 -> x0, waiting for transfers between devices: 42.9 us -> none  [the longest x12 24.7 us: from_behind(): return lax.ppermute(value, axis, pairs)]
    pallas_call x1 -> x3, Pallas kernels: 79.7 us -> 114 us  [the longest x1 79.7 us: per_device(): pl.pallas_call(functools.partial(edge_kernel, block_atoms), out_shape=(ja...]
    ppermute x20 -> x0, starting transfers between devices: 25.5 us -> none  [the longest x12 12.3 us: from_behind(): return lax.ppermute(value, axis, pairs)]
    unnamed x30 -> x31, local copies, waits for them, and re-layouts: 3.08 us -> 14.2 us
    scatter x9 -> x0, local copies, waits for them, and re-layouts: 6.38 us -> none  [the longest x3 1.69 us: move_along_y(): own_coords = own_coords.at[:, picked].set(arrived_coords)]
    gather x10 -> x0, local copies, waits for them, and re-layouts: 6.26 us -> none  [the longest x2 1.19 us: move_along_y(): arrived_rows = from_behind(own_rows[picked], 'gy', stride)]
    reshape x2, local copies, waits for them, and re-layouts: 0.05 us -> 2.54 us  [the longest x1 1.27 us: per_device(): migrate_x_slots.reshape(1, -1)]
    select_n x3 -> x0, other arithmetic: 2.2 us -> none  [the longest x1 0.76 us: move_along_x(): own_rows = own_rows.at[picked].set(arrived_rows)]
  transfers between devices with their start and end apart: 20 -> 0, of which waited for: 14 -> 0; matrix products, arithmetic and copies ran while one was open for 7% -> 0% of each run, Pallas kernels for 0% -> 0%
where the time goes in v2:
time: 134 us; the launch traced here: 133 us
  Pallas kernels  114 us (85%)
  local copies, waits for them, and re-layouts  18.8 us (14%)
    pallas_call x1, Pallas kernels, per_device(): pl.pallas_call(functools.partial(edge_kernel, block_atoms), out_shape=(ja...  79.7 us
    pallas_call x1, Pallas kernels, per_device(): pl.pallas_call(functools.partial(share_kernel, shape), out_shape=(jax.Sha...  25.2 us
    unnamed x31, local copies, waits for them, and re-layouts  14.2 us
    pallas_call x1, Pallas kernels, per_device(): pl.pallas_call(functools.partial(return_kernel, shape), out_shape=jax.Sha...  8.69 us

profile of v2, /device:TPU:0, one launch (start us, length us, event | category | flops | bytes accessed | tf_op | source)
XLA Modules:
  0.0 133.2 jit_solution(10686795136733484358)
XLA Ops:
  0.6 1.3 reshape.20.slots_x
  1.9 1.3 reshape.21.slots_y
  3.2 1.3 copy.22
  4.5 0.8 broadcast_in_dim.9.index_ref
  5.2 0.8 copy.20
  6.0 25.2 %share.1 = (f32[2816,128]{1,0:T(8,128)}, f32[512,128]{1,0:T(8,128)}, f32[3,24,128]{2,1,0:T(8,128)}, f32[8,512]{1,0:T(8,128)}) custom-call(bf16[512,128]{1,0:T(8,128)(2,1)} %bitcast.18, f32[3,512]{1,0:T(4,128)} %bitcast.21, s32[1,64]{1,0:T(1,128)} %reshape.20.slots_x, s32[1,64]{1,0:T(1,128)} %reshape.21.slots_y, s32[1,256]{1,0:T(1,128)} %bitcast.23, ...), custom_call_target="tpu_custom_call" | custom-call | tf_op jit(solution)/shard_map/share/pallas_call | solution.py:527
  31.3 1.4 %copy-done = f32[2816,128]{1,0:T(8,128)S(1)} copy-done((f32[2816,128]{1,0:T(8,128)S(1)}, f32[2816,128]{1,0:T(8,128)}, u32[]{:S(2)}) %copy-start) | copy-done | bytes 1441816
  32.6 0.9 copy-done.1
  33.6 0.8 copy-done.3
  34.3 0.8 copy-done.4
  35.1 0.8 copy-done.5
  35.9 0.8 copy-done.6
  36.6 0.8 copy-done.7
  37.4 0.8 copy-done.8
  38.1 0.8 copy-done.9
  38.9 0.7 copy-done.11
  39.6 0.7 copy-done.12
  40.3 0.7 copy-done.13
  40.9 79.7 %edges.1 = (f32[72,128]{1,0:T(8,128)S(1)}, f32[8,512]{1,0:T(8,128)S(1)}) custom-call(s32[8192]{0:T(1024)S(1)} %bitcast.15, s32[16,1,512]{2,1,0:T(1,128)S(1)} %broadcast_in_dim.9.index_ref, f32[2816,128]{1,0:T(8,128)S(1)} %copy-done, f32[512,128]{1,0:T(8,128)S(1)} %copy-done.1, f32[3,24,128]{2,1,0:T(8,128)S(1)} %copy-done.3, f32[8,512]{1,0:T(8,128)S(1)} %copy-done.11, ...), custom_call_target="tpu_custom_call" | custom-call | tf_op jit(solution)/shard_map/edges/pallas_call | solution.py:566
  120.7 0.6 copy-done.2
  121.3 0.6 copy-done.10
  121.9 8.7 %give_back.1 = f32[3,512]{1,0:T(4,128)} custom-call(f32[3,24,128]{2,1,0:T(8,128)} %bitcast.16, f32[8,512]{1,0:T(8,128)} %copy-done.10, s32[1,256]{1,0:T(1,128)} %bitcast.24), custom_call_target="tpu_custom_call" | custom-call | tf_op jit(solution)/shard_map/give_back/pallas_call | solution.py:605
  130.6 1.3 slice_bitcast_fusion
  131.9 1.3 copy.18
  (14 shorter events, 0.0 us)
Async XLA Ops:
  31.3 1.4 %copy-start = (f32[2816,128]{1,0:T(8,128)S(1)}, f32[2816,128]{1,0:T(8,128)}, u32[]{:S(2)}) copy-start(f32[2816,128]{1,0:T(8,128)} %get-tuple-element.8.table_ref) | copy-start | bytes 4325380
  32.6 0.9 copy-start.1
  33.6 0.8 copy-start.3
  34.3 0.8 copy-start.4
  35.1 0.8 copy-start.5
  35.9 0.8 copy-start.6
  36.6 0.8 copy-start.7
  37.4 0.8 copy-start.8
  38.1 0.8 copy-start.9
  38.9 0.7 copy-start.11
  39.6 0.7 copy-start.12
  40.3 0.7 copy-start.13
  120.7 0.6 copy-start.2
  121.3 0.6 copy-start.10

commit v3 on v2

--- a/solution.py
+++ b/solution.py
@@ -29,12 +29,22 @@
 
 def edge_kernel(
     block_atoms,
-    index_smem,
     index_ref,
     table_ref,
     source_ref,
     place_ref,
     own_ref,
+    radial_far,
+    environ_first_far,
+    mixing_first_far,
+    coupler_first_far,
+    environ_second_far,
+    mixing_second_far,
+    coupler_second_far,
+    readout_far,
+    scatter_ref,
+    atom_ref,
+    energy_ref,
     radial_ref,
     environ_first,
     mixing_first,
@@ -43,8 +53,9 @@
     mixing_second,
     coupler_second,
     readout_ref,
-    scatter_ref,
-    atom_ref,
+    fetch_sem,
+    index_sem,
+    index_smem,
     gathered,
     scalars,
     results,
@@ -57,21 +68,55 @@
     pick_weights,
     place_split,
 ):
-    slots_per, _, atom_count = index_ref.shape
+    slots_per, atom_count = index_ref.shape
     breadth = table_ref.shape[1]
     groups = place_ref.shape[1]
     f32 = jnp.float32
     bf16 = jnp.bfloat16
-    step = 16
+    lists = [
+        pltpu.make_async_copy(
+            index_ref.at[slot],
+            index_smem.at[pl.ds(slot * atom_count, atom_count)],
+            index_sem.at[slot],
+        )
+        for slot in range(slots_per)
+    ]
+    for fetch in lists:
+        fetch.start()
+    fetches = [
+        pltpu.make_async_copy(far, near, fetch_sem.at[n])
+        for n, (far, near) in enumerate(
+            (
+                (radial_far, radial_ref),
+                (environ_first_far, environ_first),
+                (mixing_first_far, mixing_first),
+                (coupler_first_far, coupler_first),
+                (environ_second_far, environ_second),
+                (mixing_second_far, mixing_second),
+                (coupler_second_far, coupler_second),
+                (readout_far, readout_ref),
+            )
+        )
+    ]
+    for fetch in fetches:
+        fetch.start()
+
+    for fetch in lists:
+        fetch.wait()
+    step = math.gcd(atom_count, 16)
 
     @pl.loop(0, slots_per)
     def _(slot):
         @pl.loop(0, atom_count // step)
         def _(part):
             base = pl.multiple_of(part * step, step)
+            start = slot * atom_count + base
             for u in range(step):
-                row = index_smem[slot * atom_count + base + u]
+                row = index_smem[start + u]
                 gathered[slot, pl.ds(base + u, 1), :] = table_ref[pl.ds(row, 1), :]
+
+    for fetch in fetches:
+        fetch.wait()
 
     forward_weights[0, :, :breadth] = environ_first[...]
     forward_weights[0, :, breadth:] = mixing_first[...]
@@ -105,7 +150,7 @@
     place_split[...] = jnp.concatenate([p_top, p_mid, p_low], axis=0).astype(bf16)
 
     def chosen(slot):
-        index = index_ref[slot]
+        index = index_ref[pl.ds(slot, 1), :]
         low = lax.rem(index, breadth)
         high = lax.div(index, breadth)
         rows = lax.broadcasted_iota(jnp.int32, (breadth, atom_count), 0)
@@ -113,7 +158,7 @@
         group_rows = lax.broadcasted_iota(jnp.int32, (groups, atom_count), 0)
         return (one_hot, group_rows == high)
 
-    @pl.loop(0, slots_per)
+    @pl.loop(0, slots_per, unroll=4)
     def _(slot):
         one_hot, in_group = chosen(slot)
         found = jnp.dot(place_split[...], one_hot, preferred_element_type=f32)
@@ -162,13 +207,14 @@
     def product(left, right):
         return jnp.dot(left.astype(bf16), right, preferred_element_type=f32)
 
-    @pl.loop(0, atom_count // block_atoms)
+    @pl.loop(0, atom_count // block_atoms, unroll=1)
     def _(block):
         first = pl.multiple_of(block * block_atoms, block_atoms)
         atoms = pl.ds(first, block_atoms)
         narrow = scalars[:, atoms, :]
         radial = product(narrow.reshape(edges, breadth), radial_in[...]).reshape(cube)
-        paired = gathered[:, atoms, :] + source_ref[atoms, :][None] + radial
+        rows = gathered[:, atoms, :]
+        paired = rows + source_ref[atoms, :][None] + radial
         gate = sigmoid(paired)
         value = paired * gate
         slopes = [gate + value * (1.0 - gate)]
@@ -236,8 +282,9 @@
 
     scatter_ref[...] = jnp.zeros(scatter_ref.shape, f32)
     atom_ref[...] = jnp.zeros(atom_ref.shape, f32)
-
-    @pl.loop(0, slots_per)
+    energy_ref[...] = jnp.zeros(energy_ref.shape, f32)
+
+    @pl.loop(0, slots_per, unroll=1)
     def _(slot):
         flat = results[slot].T
         data = saved[slot]
@@ -279,8 +326,8 @@
                 piece, one_hot, (((1,), (1,)), ((), ())), preferred_element_type=f32
             )
         blank = jnp.zeros_like(sine)
-        atom_rows = atom_rows + [edge_energy * smooth] + [blank] * 4
-        atom_ref[...] += jnp.concatenate(atom_rows, axis=0)
+        atom_ref[...] += jnp.concatenate(atom_rows + [blank] * 5, axis=0)
+        energy_ref[...] += edge_energy * smooth
 
 
 def others(shape):
@@ -319,12 +366,14 @@
     slots_x,
     slots_y,
     ghosts,
+    neighbours,
     source_weight,
     target_weight,
     table_ref,
     source_ref,
     place_ref,
     own_ref,
+    index_ref,
     holding,
     leaving,
     arriving,
@@ -343,7 +392,8 @@
     bf16 = jnp.bfloat16
     mesh_ids = pl.DeviceIdType.MESH
     count, breadth = features.shape
-    sent = slots_x.shape[1] // 2
+    sent = slots_x.shape[1]
+    slots_per = neighbours.shape[1]
     ghost_count = ghosts.shape[1]
     at, steps = others(shape)
     barrier = greet(shape)
@@ -355,18 +405,23 @@
     pieces.append(jnp.zeros((breadth - 24, count), f32))
     holding[:, :breadth] = features[...]
     holding[:, breadth:] = jnp.concatenate(pieces, axis=0).T.astype(bf16)
-    both = jnp.concatenate([slots_x[...], slots_y[...]], axis=1)
+    slots_x = jnp.concatenate([slots_x[0:1, :], slots_x[1:2, :]], axis=1)
+    slots_y = jnp.concatenate([slots_y[0:1, :], slots_y[1:2, :]], axis=1)
+    both = jnp.concatenate([slots_x, slots_y], axis=1)
     picks = hot_columns(both, count).T.astype(bf16)
     ghost_hot = hot_columns(ghosts[...], count)
     ghost_picks = ghost_hot.T.astype(bf16)
     ghost_hot = ghost_hot.astype(bf16)
+    listed = neighbours[...].astype(f32)
+    listed = jnp.concatenate([listed, jnp.zeros((count, breadth - slots_per), f32)], axis=1)
+    index_ref[...] = listed.T[:slots_per].astype(jnp.int32)
 
     for axis, slots in ((0, slots_x), (1, slots_y)):
         chosen = picks[2 * sent * axis : 2 * sent * (axis + 1)]
         payload = jnp.dot(chosen, holding[...], preferred_element_type=f32).astype(bf16)
         leaving[axis, 0] = payload[:sent]
         leaving[axis, 1] = payload[sent:]
-        put = hot_columns(slots[...], count)
+        put = hot_columns(slots, count)
         hit = jnp.max(put, axis=1, keepdims=True) > 0.5
         put = put.astype(bf16)
         if axis == 0:
@@ -522,18 +577,18 @@
     f32 = jnp.float32
     bf16 = jnp.bfloat16
     vmem = pl.BlockSpec(memory_space=pltpu.VMEM)
-    smem = pl.BlockSpec(memory_space=pltpu.SMEM)
     dma = pltpu.SemaphoreType.DMA
-    table, source_rows, places, own = pl.pallas_call(
+    table, source_rows, places, own, by_slot = pl.pallas_call(
         functools.partial(share_kernel, shape),
         out_shape=(
             jax.ShapeDtypeStruct((total_rows, breadth), f32),
             jax.ShapeDtypeStruct((count, breadth), f32),
             jax.ShapeDtypeStruct((3, groups, breadth), f32),
             jax.ShapeDtypeStruct((8, count), f32),
+            jax.ShapeDtypeStruct((slots_per, count), jnp.int32),
         ),
-        in_specs=[vmem] * 7,
-        out_specs=(vmem,) * 4,
+        in_specs=[vmem] * 8,
+        out_specs=(vmem,) * 5,
         scratch_shapes=[
             pltpu.VMEM((count, 2 * breadth), bf16),
             pltpu.VMEM((2, 2, sent, 2 * breadth), bf16),
@@ -549,29 +604,39 @@
             dma((9,)),
             dma((9,)),
         ],
-        compiler_params=pltpu.CompilerParams(collective_id=0, has_side_effects=True),
+        compiler_params=pltpu.CompilerParams(collective_id=0, has_side_effects=True, vmem_limit_bytes=14 * 1024 * 1024
+        ),
         name="share",
     )(
         features,
         coords,
-        migrate_x_slots.reshape(1, -1),
-        migrate_y_slots.reshape(1, -1),
+        migrate_x_slots[0, 0],
+        migrate_y_slots[0, 0],
         ghosts,
+        neighbours,
         source_weight,
         target_weight,
     )
-    by_slot = neighbours.T
-    block_atoms = math.gcd(count, 16)
+    block_atoms = math.gcd(count, 64)
     cube = (slots_per, count, breadth)
-    scattered, by_atom = pl.pallas_call(
+    scattered, by_atom, energies = pl.pallas_call(
         functools.partial(edge_kernel, block_atoms),
         out_shape=(
             jax.ShapeDtypeStruct((3 * groups, breadth), f32),
             jax.ShapeDtypeStruct((8, count), f32),
+            jax.ShapeDtypeStruct((1, count), f32),
         ),
-        in_specs=[smem] + [vmem] * 13,
-        out_specs=(vmem, vmem),
+        in_specs=[vmem] * 5 + [pl.BlockSpec(memory_space=pl.ANY)] * 8,
+        out_specs=(vmem,) * 3,
         scratch_shapes=[
+            pltpu.VMEM(radial_weight.shape, f32),
+        ]
+        + [pltpu.VMEM((breadth, breadth), bf16)] * 6
+        + [
+            pltpu.VMEM((1, breadth), bf16),
+            dma((8,)),
+            dma((slots_per,)),
+            pltpu.SMEM((slots_per * count,), jnp.int32),
             pltpu.VMEM(cube, f32),
             pltpu.VMEM(cube, f32),
             pltpu.VMEM(cube, f32),
@@ -584,11 +649,10 @@
             pltpu.VMEM((4 * breadth, breadth), bf16),
             pltpu.VMEM((9 * groups, breadth), bf16),
         ],
-        compiler_params=pltpu.CompilerParams(vmem_limit_bytes=48 * 1024 * 1024),
+        compiler_params=pltpu.CompilerParams(vmem_limit_bytes=24 * 1024 * 1024),
         name="edges",
     )(
-        by_slot.reshape(-1),
-        by_slot[:, None, :],
+        by_slot,
         table,
         source_rows,
         places,
@@ -613,10 +677,11 @@
             dma((9,)),
             dma((9,)),
         ],
-        compiler_params=pltpu.CompilerParams(collective_id=1, has_side_effects=True),
+        compiler_params=pltpu.CompilerParams(collective_id=1, has_side_effects=True, vmem_limit_bytes=6 * 1024 * 1024
+        ),
         name="give_back",
     )(scattered.reshape(3, groups, breadth), by_atom, ghosts)
-    return (forces[None, None], by_atom[3][None, None])
+    return (forces[None, None], energies[None])
 
 
 def solution(mesh):

time: 134 us -> 98.9 us (0.74)
  Pallas kernels: 114 us -> 84.8 us
  local copies, waits for them, and re-layouts: 18.8 us -> 12.5 us
    pallas_call x1, Pallas kernels: 79.7 us -> 54.3 us  [per_device(): pl.pallas_call(functools.partial(edge_kernel, block_atoms), out_shape=(ja...]
    reshape x2 -> x0, local copies, waits for them, and re-layouts: 2.54 us -> none  [the longest x1 1.27 us: per_device(): migrate_x_slots.reshape(1, -1)]
    pallas_call x1, Pallas kernels: 25.2 us -> 23.1 us  [per_device(): pl.pallas_call(functools.partial(share_kernel, shape), out_shape=(jax.Sha...]
    unnamed x31 -> x33, local copies, waits for them, and re-layouts: 14.2 us -> 12.5 us
where the time goes in v3:
time: 98.9 us; the launch traced here: 98 us
  Pallas kernels  84.8 us (86%)
  local copies, waits for them, and re-layouts  12.5 us (13%)
    pallas_call x1, Pallas kernels, per_device(): pl.pallas_call(functools.partial(edge_kernel, block_atoms), out_shape=(ja...  54.3 us
    pallas_call x1, Pallas kernels, per_device(): pl.pallas_call(functools.partial(share_kernel, shape), out_shape=(jax.Sha...  23.1 us
    unnamed x33, local copies, waits for them, and re-layouts  12.5 us
    pallas_call x1, Pallas kernels, per_device(): pl.pallas_call(functools.partial(return_kernel, shape), out_shape=jax.Sha...  7.39 us

profile of v3, /device:TPU:0, one launch (start us, length us, event | category | flops | bytes accessed | tf_op | source)
XLA Modules:
  0.0 98.0 jit_solution(14558425195539997532)
XLA Ops:
  0.6 0.0 copy-start.11
  0.6 0.7 copy.22
  1.3 0.9 copy.18
  2.2 0.0 copy-start
  2.2 0.9 copy-done
  3.1 0.8 copy-done.7
  3.9 0.8 copy-done.8
  4.7 0.7 copy-done.10
  5.3 0.7 copy-done.12
  6.0 0.7 copy-done.13
  6.7 23.1 %share.1 = (f32[2816,128]{1,0:T(8,128)S(1)}, f32[512,128]{1,0:T(8,128)S(1)}, f32[3,24,128]{2,1,0:T(8,128)S(1)}, f32[8,512]{1,0:T(8,128)S(1)}, s32[16,512]{1,0:T(8,128)S(1)}) custom-call(bf16[512,128]{1,0:T(8,128)(2,1)S(1)} %bitcast.13, f32[3,512]{1,0:T(4,128)S(1)} %bitcast.15, s32[2,32]{1,0:T(2,128)S(1)} %bitcast.19, s32[2,32]{1,0:T(2,128)S(1)} %bitcast.20, ...), custom_call_target="tpu_custom_call" | custom-call | tf_op jit(solution)/shard_map/share/pallas_call | solution.py:581
  29.8 0.0 copy-start.1
  29.8 0.7 copy-done.1
  30.5 0.8 copy-done.2
  31.3 0.8 copy-done.3
  32.0 0.8 copy-done.4
  32.8 0.8 copy-done.5
  33.5 0.8 copy-done.6
  34.3 0.7 copy-done.9
  35.0 0.7 copy-done.14
  35.6 54.3 %edges.1 = (f32[72,128]{1,0:T(8,128)S(1)}, f32[8,512]{1,0:T(8,128)S(1)}, f32[1,512]{1,0:T(1,128)}) custom-call(s32[16,512]{1,0:T(8,128)S(1)} %get-tuple-element.10.index_ref, f32[2816,128]{1,0:T(8,128)S(1)} %get-tuple-element.11.table_ref, f32[512,128]{1,0:T(8,128)S(1)} %get-tuple-element.12.source_ref, f32[3,24,128]{2,1,0:T(8,128)S(1)} %get-tuple-element.13.place_ref, ...), custom_call_target="tpu_custom_call" | custom-call | tf_op jit(solution)/shard_map/edges/pallas_call | solution.py:622
  90.0 0.0 copy-done.11
  90.0 7.4 %give_back.1 = f32[3,512]{1,0:T(4,128)S(1)} custom-call(f32[3,24,128]{2,1,0:T(8,128)S(1)} %bitcast.14, f32[8,512]{1,0:T(8,128)S(1)} %get-tuple-element.16.by_atom, s32[1,256]{1,0:T(1,128)S(1)} %bitcast.18), custom_call_target="tpu_custom_call" | custom-call | tf_op jit(solution)/shard_map/give_back/pallas_call | solution.py:669
  97.4 0.6 copy.19
  (12 shorter events, 0.0 us)
Async XLA Ops:
  0.6 89.4 %copy-start.11 = (s32[1,1,256]{2,1,0:T(1,128)S(1)}, s32[1,1,256]{2,1,0:T(1,128)}, u32[]{:S(2)}) copy-start(s32[1,1,256]{2,1,0:T(1,128)} %param.20) | copy-start | bytes 3076
  2.2 0.9 copy-start
  3.1 0.8 copy-start.7
  3.9 0.8 copy-start.8
  4.7 0.7 copy-start.10
  5.3 0.7 copy-start.12
  6.0 0.7 copy-start.13
  29.8 0.8 copy-start.1
  30.5 0.8 copy-start.2
  31.3 0.8 copy-start.3
  32.0 0.8 copy-start.4
  32.8 0.8 copy-start.5
  33.5 0.8 copy-start.6
  34.3 0.7 copy-start.9
  35.0 0.7 copy-start.14

commit v4 on v3

--- a/solution.py
+++ b/solution.py
@@ -361,19 +361,26 @@
 
 def share_kernel(
     shape,
-    features,
+    features_far,
     coords,
-    slots_x,
-    slots_y,
-    ghosts,
+    slots_x_far,
+    slots_y_far,
+    ghosts_far,
     neighbours,
-    source_weight,
-    target_weight,
+    source_weight_far,
+    target_weight_far,
     table_ref,
     source_ref,
     place_ref,
     own_ref,
     index_ref,
+    features,
+    slots_x,
+    slots_y,
+    ghosts,
+    source_weight,
+    target_weight,
+    fetch_sem,
     holding,
     leaving,
     arriving,
@@ -397,14 +404,31 @@
     ghost_count = ghosts.shape[1]
     at, steps = others(shape)
     barrier = greet(shape)
+    fetches = [
+        pltpu.make_async_copy(far, near, fetch_sem.at[n])
+        for n, (far, near) in enumerate(
+            (
+                (features_far, features),
+                (slots_x_far, slots_x),
+                (slots_y_far, slots_y),
+                (ghosts_far, ghosts),
+                (source_weight_far, source_weight),
+                (target_weight_far, target_weight),
+            )
+        )
+    ]
+    for fetch in fetches:
+        fetch.start()
 
     blank = jnp.zeros((5, count), f32)
     pieces = []
     for piece in split_three(coords[...]):
         pieces += [piece, blank]
     pieces.append(jnp.zeros((breadth - 24, count), f32))
+    holding[:, breadth:] = jnp.concatenate(pieces, axis=0).T.astype(bf16)
+    for fetch in fetches:
+        fetch.wait()
     holding[:, :breadth] = features[...]
-    holding[:, breadth:] = jnp.concatenate(pieces, axis=0).T.astype(bf16)
     slots_x = jnp.concatenate([slots_x[0:1, :], slots_x[1:2, :]], axis=1)
     slots_y = jnp.concatenate([slots_y[0:1, :], slots_y[1:2, :]], axis=1)
     both = jnp.concatenate([slots_x, slots_y], axis=1)
@@ -577,6 +601,7 @@
     f32 = jnp.float32
     bf16 = jnp.bfloat16
     vmem = pl.BlockSpec(memory_space=pltpu.VMEM)
+    hbm = pl.BlockSpec(memory_space=pltpu.HBM)
     dma = pltpu.SemaphoreType.DMA
     table, source_rows, places, own, by_slot = pl.pallas_call(
         functools.partial(share_kernel, shape),
@@ -587,9 +612,16 @@
             jax.ShapeDtypeStruct((8, count), f32),
             jax.ShapeDtypeStruct((slots_per, count), jnp.int32),
         ),
-        in_specs=[vmem] * 8,
+        in_specs=[hbm, vmem, hbm, hbm, hbm, vmem, hbm, hbm],
         out_specs=(vmem,) * 5,
         scratch_shapes=[
+            pltpu.VMEM((count, breadth), bf16),
+            pltpu.VMEM((2, sent), jnp.int32),
+            pltpu.VMEM((2, sent), jnp.int32),
+            pltpu.VMEM((1, ghost_count), jnp.int32),
+            pltpu.VMEM((breadth, breadth), bf16),
+            pltpu.VMEM((breadth, breadth), bf16),
+            dma((6,)),
             pltpu.VMEM((count, 2 * breadth), bf16),
             pltpu.VMEM((2, 2, sent, 2 * breadth), bf16),
             pltpu.VMEM((2, 2, sent, 2 * breadth), bf16),
@@ -604,7 +636,7 @@
             dma((9,)),
             dma((9,)),
         ],
-        compiler_params=pltpu.CompilerParams(collective_id=0, has_side_effects=True, vmem_limit_bytes=14 * 1024 * 1024
+        compiler_params=pltpu.CompilerParams(collective_id=0, has_side_effects=True, vmem_limit_bytes=67043328
         ),
         name="share",
     )(
@@ -626,7 +658,7 @@
             jax.ShapeDtypeStruct((8, count), f32),
             jax.ShapeDtypeStruct((1, count), f32),
         ),
-        in_specs=[vmem] * 5 + [pl.BlockSpec(memory_space=pl.ANY)] * 8,
+        in_specs=[vmem] * 5 + [pl.BlockSpec(memory_space=pltpu.HBM)] * 8,
         out_specs=(vmem,) * 3,
         scratch_shapes=[
             pltpu.VMEM(radial_weight.shape, f32),
@@ -649,7 +681,7 @@
             pltpu.VMEM((4 * breadth, breadth), bf16),
             pltpu.VMEM((9 * groups, breadth), bf16),
         ],
-        compiler_params=pltpu.CompilerParams(vmem_limit_bytes=24 * 1024 * 1024),
+        compiler_params=pltpu.CompilerParams(vmem_limit_bytes=67043328),
         name="edges",
     )(
         by_slot,
@@ -677,7 +709,7 @@
             dma((9,)),
             dma((9,)),
         ],
-        compiler_params=pltpu.CompilerParams(collective_id=1, has_side_effects=True, vmem_limit_bytes=6 * 1024 * 1024
+        compiler_params=pltpu.CompilerParams(collective_id=1, has_side_effects=True, vmem_limit_bytes=67043328
         ),
         name="give_back",
     )(scattered.reshape(3, groups, breadth), by_atom, ghosts)

time: 98.9 us -> 95.2 us (0.963)
  local copies, waits for them, and re-layouts: 12.5 us -> 4.17 us
  Pallas kernels: 84.8 us -> 90 us
    unnamed x33 -> x3, local copies, waits for them, and re-layouts: 12.5 us -> 4.17 us
    pallas_call x1, Pallas kernels: 23.1 us -> 25.3 us  [per_device(): pl.pallas_call(functools.partial(share_kernel, shape), out_shape=(jax.Sha...]
    pallas_call x1, Pallas kernels: 54.3 us -> 56 us  [per_device(): pl.pallas_call(functools.partial(edge_kernel, block_atoms), out_shape=(ja...]
    pallas_call x1, Pallas kernels: 7.39 us -> 8.69 us  [per_device(): pl.pallas_call(functools.partial(return_kernel, shape), out_shape=jax.Sha...]
where the time goes in v4:
time: 95.2 us; the launch traced here: 94.8 us
  Pallas kernels  90 us (95%)
  local copies, waits for them, and re-layouts  4.17 us (4%)
    pallas_call x1, Pallas kernels, per_device(): pl.pallas_call(functools.partial(edge_kernel, block_atoms), out_shape=(ja...  56 us
    pallas_call x1, Pallas kernels, per_device(): pl.pallas_call(functools.partial(share_kernel, shape), out_shape=(jax.Sha...  25.3 us
    pallas_call x1, Pallas kernels, per_device(): pl.pallas_call(functools.partial(return_kernel, shape), out_shape=jax.Sha...  8.69 us
    unnamed x3, local copies, waits for them, and re-layouts  4.17 us

profile of v4, /device:TPU:0, one launch (start us, length us, event | category | flops | bytes accessed | tf_op | source)
XLA Modules:
  0.0 94.8 jit_solution(8046653664273864387)
XLA Ops:
  0.6 1.3 %copy.22 = f32[1,1,3,512]{3,2,1,0:T(4,128)} copy(f32[1,1,3,512]{3,1,2,0:T(1,128)} %param.17) | data formatting | bytes 12288
  1.9 1.6 %copy.18 = s32[1,1,512,16]{3,2,1,0:T(8,128)} copy(s32[1,1,512,16]{2,3,1,0:T(8,128)} %param.21) | data formatting | bytes 65536 | tf_op args[5]
  3.5 25.3 %share.1 = (f32[2816,128]{1,0:T(8,128)}, f32[512,128]{1,0:T(8,128)}, f32[3,24,128]{2,1,0:T(8,128)}, f32[8,512]{1,0:T(8,128)}, s32[16,512]{1,0:T(8,128)}) custom-call(bf16[512,128]{1,0:T(8,128)(2,1)} %bitcast.13, f32[3,512]{1,0:T(4,128)} %bitcast.15, s32[2,32]{1,0:T(2,128)} %bitcast.19, s32[2,32]{1,0:T(2,128)} %bitcast.20, s32[1,256]{1,0:T(1,128)} %bitcast.17, ...), custom_call_target="tpu_custom_call" | custom-call | tf_op jit(solution)/shard_map/share/pallas_call | solution.py:606
  28.8 56.0 %edges.1 = (f32[72,128]{1,0:T(8,128)}, f32[8,512]{1,0:T(8,128)}, f32[1,512]{1,0:T(1,128)}) custom-call(s32[16,512]{1,0:T(8,128)} %get-tuple-element.10.index_ref, f32[2816,128]{1,0:T(8,128)} %get-tuple-element.11.table_ref, f32[512,128]{1,0:T(8,128)} %get-tuple-element.12.source_ref, f32[3,24,128]{2,1,0:T(8,128)} %get-tuple-element.13.place_ref, ...), custom_call_target="tpu_custom_call" | custom-call | tf_op jit(solution)/shard_map/edges/pallas_call | solution.py:654
  84.8 8.7 %give_back.1 = f32[3,512]{1,0:T(4,128)} custom-call(f32[3,24,128]{2,1,0:T(8,128)} %bitcast.14, f32[8,512]{1,0:T(8,128)} %get-tuple-element.16.by_atom, s32[1,256]{1,0:T(1,128)} %bitcast.18), custom_call_target="tpu_custom_call" | custom-call | tf_op jit(solution)/shard_map/give_back/pallas_call | solution.py:701
  93.5 1.3 %copy.19 = f32[1,1,3,512]{3,1,2,0:T(1,128)} copy(f32[1,1,3,512]{3,2,1,0:T(4,128)} %bitcast.16) | data formatting | bytes 12288
